TPU v7x, 768 devices: a whole 4x8x12 slice. The times are simulated.
768 devices in a mesh: wide: 192 (over z, y, x_lo), narrow: 4 (over x_hi, core).
Axes of the slice: x: 4 (x_hi: 2, x_lo: 2; x = x_hi * 2 + x_lo), y: 8, z: 12, core: 2. Of those that a mesh axis runs over, the one named last changes fastest.
Arguments:
- events: bfloat16 [98304, 1024], P(('wide', 'narrow')), may hold values from -6 to 6
- buckets: int32 [98304], P('wide'), may hold values from 0 to 63
- counts: int32 [192], replicated, may hold values from 256 to 512, as said below
- prior_keys: bfloat16 [1024, 1024], P(None, 'narrow'), may hold values from -6 to 6
- prior_values: bfloat16 [1024, 1024], P(None, 'narrow'), may hold values from -6 to 6
- prior_buckets: int32 [1024], replicated, may hold values from 0 to 63
- w_input: bfloat16 [1024, 4096], replicated, may hold values from -0.1875 to 0.1875
- w_output: bfloat16 [1024, 1024], replicated, may hold values from -0.1875 to 0.1875
- time_bias: float32 [64, 16], replicated, may hold values from -4 to 4
Outputs:
- result: bfloat16 [98304, 1024], P(('wide', 'narrow'))
Inputs may be any that keep to these rules, and one draw needn't show every extreme that they name: `counts`: some block is full in every draw.
All inputs are finite; a program needn't handle non-finite values.
Results may differ from a plain program's by a relative error of at most 0.0068.
Values may be sent and summed in bfloat16 or wider, within the bound.
No kernel may reach another device: no remote copies, remote signals or barrier semaphores. Data moves between devices by JAX's collectives and lax.ppermute only.
A program may use at most 64 MiB of HBM per device.

v0:
```python
import jax
import jax.numpy as jnp
from jax import lax
from jax.sharding import PartitionSpec as P

HEAD_DIM = 64
NB = 64


def passed_along(block, axis, distance):
    devices = range(lax.axis_size(axis))
    route = [(i - distance, i) for i in devices if i - distance in devices]
    return lax.ppermute(block, axis, route)


def for_sending(value):

    def short(part):
        return part.astype(jnp.bfloat16) if part.dtype == jnp.float32 else part

    return jax.tree.map(short, value)


def layer_norm(values):
    mean = jnp.mean(values, axis=-1, keepdims=True)
    centred = values - mean
    var = jnp.mean(centred * centred, axis=-1, keepdims=True)
    return centred * lax.rsqrt(var + 1e-05)


def per_device(
    events, buckets, counts, prior_keys, prior_values, prior_buckets, w_input, w_output, time_bias
):
    width = events.shape[1]
    local_width = width // lax.axis_size("narrow")
    head_index = lax.axis_index("narrow")
    normed = layer_norm(events.astype(jnp.float32)).astype(jnp.bfloat16)
    proj = jax.nn.silu(jnp.dot(normed, w_input, preferred_element_type=jnp.float32)).astype(
        jnp.bfloat16
    )
    gate_u = proj[:, 0:width]
    values = proj[:, width : 2 * width]
    queries = proj[:, 2 * width : 3 * width]
    keys = proj[:, 3 * width : 4 * width]
    queries, keys, values = (
        lax.all_to_all(queries, "narrow", split_axis=1, concat_axis=0, tiled=True),
        lax.all_to_all(keys, "narrow", split_axis=1, concat_axis=0, tiled=True),
        lax.all_to_all(values, "narrow", split_axis=1, concat_axis=0, tiled=True),
    )
    block_len = queries.shape[0]
    local_heads = local_width // HEAD_DIM
    wide_index = lax.axis_index("wide")
    first = wide_index == 0
    cached_buckets = prior_buckets.astype(jnp.bfloat16)
    far_cache = (prior_keys[0:block_len], prior_values[0:block_len], cached_buckets[0:block_len])
    near_cache = (prior_keys[block_len:], prior_values[block_len:], cached_buckets[block_len:])
    resident = (keys, values, buckets.astype(jnp.bfloat16))
    shifted = passed_along((resident[0], resident[1], resident[2]), "wide", 1)
    previous = tuple((jnp.where(first, near_cache[idx], shifted[idx]) for idx in range(3)))
    relayed = jax.tree.map(
        lambda part, own: part.astype(own.dtype),
        passed_along(for_sending(previous), "wide", 1),
        previous,
    )
    earlier = tuple((jnp.where(first, far_cache[idx], relayed[idx]) for idx in range(3)))
    key_rows = jnp.concatenate([earlier[0], previous[0], keys], axis=0).reshape(
        3 * block_len, local_heads, HEAD_DIM
    )
    value_rows = jnp.concatenate([earlier[1], previous[1], values], axis=0).reshape(
        3 * block_len, local_heads, HEAD_DIM
    )
    key_buckets = jnp.concatenate([earlier[2], previous[2], resident[2]], axis=0).astype(jnp.int32)
    count_own = jnp.take(counts, wide_index)
    count_prev = jnp.where(
        wide_index >= 1, jnp.take(counts, jnp.maximum(wide_index - 1, 0)), block_len
    )
    count_far = jnp.where(
        wide_index >= 2, jnp.take(counts, jnp.maximum(wide_index - 2, 0)), block_len
    )
    rows = jnp.arange(block_len, dtype=jnp.int32)
    cols = jnp.arange(3 * block_len, dtype=jnp.int32)
    col_block = cols // block_len
    col_rest = cols % block_len
    key_count = jnp.where(
        col_block == 0, count_far, jnp.where(col_block == 1, count_prev, count_own)
    )
    valid = col_rest < key_count
    causal = (col_block[None, :] < 2) | (col_rest[None, :] <= rows[:, None])
    mask = valid[None, :] & causal
    bucket_ids = jnp.arange(NB, dtype=jnp.int32)
    query_hot = (buckets[:, None] == bucket_ids[None, :]).astype(jnp.float32)
    key_hot = (key_buckets[:, None] == bucket_ids[None, :]).astype(jnp.float32)
    bias_local = lax.dynamic_slice_in_dim(time_bias, head_index * local_heads, local_heads, 1)
    pair_gap = jnp.abs(bucket_ids[:, None] - bucket_ids[None, :])
    gap_hot = (pair_gap[:, :, None] == bucket_ids[None, None, :]).astype(jnp.float32)
    pair_table = jnp.einsum("abn,nh->hab", gap_hot, bias_local, precision=lax.Precision.HIGHEST)
    query_heads = queries.reshape(block_len, local_heads, HEAD_DIM).transpose(1, 0, 2)
    key_heads = key_rows.transpose(1, 0, 2)
    value_heads = value_rows.transpose(1, 0, 2)

    def one_head(inputs):
        query_head, key_head, value_head, table_head = inputs
        scores = (
            lax.dot_general(
                query_head, key_head, (((1,), (1,)), ((), ())), preferred_element_type=jnp.float32
            )
            * 0.125
        )
        query_bias = jnp.dot(query_hot, table_head, precision=lax.Precision.HIGHEST)
        bias_block = lax.dot_general(
            query_bias, key_hot, (((1,), (1,)), ((), ())), precision=lax.Precision.HIGHEST
        )
        scores = scores + bias_block
        weight = jnp.where(mask, jax.nn.silu(scores), 0.0).astype(jnp.bfloat16)
        return jnp.dot(weight, value_head, preferred_element_type=jnp.float32).astype(jnp.bfloat16)

    attended = lax.map(one_head, (query_heads, key_heads, value_heads, pair_table))
    attended = attended.transpose(1, 0, 2).reshape(block_len, local_width)
    attended = lax.all_to_all(attended, "narrow", split_axis=0, concat_axis=1, tiled=True)
    gated = (layer_norm(attended.astype(jnp.float32)) * gate_u.astype(jnp.float32)).astype(
        jnp.bfloat16
    )
    mixed = events.astype(jnp.float32) + jnp.dot(
        gated, w_output, preferred_element_type=jnp.float32
    )
    return mixed.astype(jnp.bfloat16)


def solution(mesh):
    placed = (
        P(("wide", "narrow"), None),
        P("wide"),
        P(),
        P(None, "narrow"),
        P(None, "narrow"),
        P(),
        P(),
        P(),
        P(),
    )
    return jax.shard_map(
        per_device,
        mesh=mesh,
        in_specs=placed,
        out_specs=P(("wide", "narrow"), None),
        check_vma=False,
    )
```

profile of v0, /device:TPU:512, one launch (start us, length us, event | category | flops | bytes accessed | tf_op | source)
XLA Modules:
  0.0 135.7 jit_solution(5979486407518933643)
XLA Ops:
  0.0 1.2 convert_reduce_fusion.1
  1.2 1.2 fusion.28
  2.4 4.9 %multiply_convert_fusion = bf16[128,4096]{1,0:T(8,128)(2,1)S(1)} fusion(bf16[1024,4096]{1,0:T(8,128)(2,1)} %param.17, bf16[128,1024]{1,0:T(8,128)(2,1)} %param.11, f32[128]{0:T(128)S(1)} %add_rsqrt_fusion.1, f32[128]{0:T(128)S(1)} %broadcast_multiply_fusion.1), kind=kOutput, calls=%fused_computation.29 | convolution fusion | flops 1076887552 | bytes 9700352 | tf_op jit(solution)/shard_map/dot_general | solution.py:38
  7.3 1.0 copy-done.2
  8.4 0.8 copy.64
  9.2 4.3 %all-to-all-start.2 = ((bf16[128,4,256]{0,2,1:T(8,128)(2,1)}), bf16[128,4,256]{0,2,1:T(8,128)(2,1)S(1)}, u32[]{:S(2)}, u32[]{:S(2)}) async-start(bf16[128,4,256]{0,2,1:T(8,128)(2,1)} %bitcast.9), calls=%async_computation.2 | async-start | bytes 524288 | tf_op jit(solution)/shard_map/all_to_all | solution.py:48
  14.0 2.5 %collective-permute-start.2 = (bf16[512]{0:T(512)(128)(2,1)}, bf16[512]{0:T(512)(128)(2,1)}, u32[]{:S(2)}, u32[]{:S(2)}) collective-permute-start(bf16[512]{0:T(512)(128)(2,1)} %convert_element_type.64), channel_id=1, source_target_pairs={{0,4},{4,8},{8,12},{12,16},{16,20},{20,24},{24,28},{28,32},{32,36}... | collective-permute-start | bytes 3080 | tf_op jit(solution)/shard_map/ppermute | solution.py:13
  17.2 0.8 fusion.53
  18.0 1.1 fusion.54
  21.6 3.5 %fusion.23 = f32[4,64,64]{2,0,1:T(4,128)S(1)} fusion(s32[64,64]{1,0:T(8,128)} %subtract_abs_fusion, f32[64,16]{0,1:T(8,128)} %param.19, s32[]{:T(128)S(6)} %select_n.113), kind=kOutput, calls=%fused_computation.30 | convolution fusion | flops 12845056 | bytes 100356 | tf_op jit(solution)/shard_map/abn,nh->hab/dot_general | solution.py:96
  25.7 1.8 %copy.72 = bf16[512,256]{0,1:T(8,128)(2,1)} copy(bf16[512,256]{1,0:T(8,128)(2,1)} %get-tuple-element.187) | data formatting | bytes 524288
  27.5 1.8 %copy.71 = bf16[512,256]{0,1:T(8,128)(2,1)} copy(bf16[512,256]{1,0:T(8,128)(2,1)} %get-tuple-element.186) | data formatting | bytes 524288
  29.3 0.9 copy.63
  30.2 0.8 copy.70
  31.0 0.8 copy.69
  32.6 0.9 copy.62
  33.4 1.3 slice_select_fusion
  34.7 4.3 %collective-permute-start.3 = (bf16[512]{0:T(512)(128)(2,1)}, bf16[512]{0:T(512)(128)(2,1)}, u32[]{:S(2)}, u32[]{:S(2)}) collective-permute-start(bf16[512]{0:T(512)(128)(2,1)} %slice_select_fusion), channel_id=1, source_target_pairs={{0,4},{4,8},{8,12},{12,16},{16,20},{20,24},{24,28},{28,32},{32,36}... | collective-permute-start | bytes 3080 | tf_op jit(solution)/shard_map/ppermute | solution.py:13
  39.0 4.8 %all-to-all-start.1 = ((bf16[128,4,256]{0,2,1:T(8,128)(2,1)}), bf16[128,4,256]{0,2,1:T(8,128)(2,1)S(1)}, u32[]{:S(2)}, u32[]{:S(2)}) async-start(bf16[128,4,256]{0,2,1:T(8,128)(2,1)} %bitcast.3), calls=%async_computation.1 | async-start | bytes 524288 | tf_op jit(solution)/shard_map/all_to_all | solution.py:47
  43.9 2.5 %collective-permute-start.4 = (bf16[512,256]{0,1:T(8,128)(2,1)S(1)}, bf16[512,256]{0,1:T(8,128)(2,1)}, u32[]{:S(2)}, u32[]{:S(2)}) collective-permute-start(bf16[512,256]{0,1:T(8,128)(2,1)S(1)} %copy_bitcast_fusion), channel_id=1, source_target_pairs={{0,4},{4,8},{8,12},{12,16},{16,20},{20,24},{24,28},{28,32},{32,36}... | collective-permute-start | bytes 786440 | tf_op jit(solution)/shard_map/ppermute | solution.py:13
  46.4 5.1 %all-to-all-done.1 = bf16[128,4,256]{0,2,1:T(8,128)(2,1)S(1)} async-done(((bf16[128,4,256]{0,2,1:T(8,128)(2,1)}), bf16[128,4,256]{0,2,1:T(8,128)(2,1)S(1)}, u32[]{:S(2)}, u32[]{:S(2)}) %all-to-all-start.1) | async-done | bytes 262176 | tf_op jit(solution)/shard_map/all_to_all | solution.py:47
  51.5 3.4 %all-to-all-start = ((bf16[128,4,256]{0,2,1:T(8,128)(2,1)}), bf16[128,4,256]{0,2,1:T(8,128)(2,1)S(1)}, u32[]{:S(2)}, u32[]{:S(2)}) async-start(bf16[128,4,256]{0,2,1:T(8,128)(2,1)} %bitcast), calls=%async_computation | async-start | bytes 524288 | tf_op jit(solution)/shard_map/all_to_all | solution.py:46
  55.0 2.3 %collective-permute-start = (bf16[512,256]{0,1:T(8,128)(2,1)S(1)}, bf16[512,256]{0,1:T(8,128)(2,1)S(1)}, u32[]{:S(2)}, u32[]{:S(2)}) collective-permute-start(bf16[512,256]{0,1:T(8,128)(2,1)S(1)} %copy_bitcast_fusion.1), channel_id=1, source_target_pairs={{0,4},{4,8},{8,12},{12,16},{16,20},{20,24},{24,28},{28,32},{32,36}... | collective-permute-start | bytes 786440 | tf_op jit(solution)/shard_map/ppermute | solution.py:13
  58.0 0.9 collective-permute-done.4
  58.9 1.0 broadcast_select_fusion.1
  59.9 3.6 %collective-permute-start.5 = (bf16[512,256]{0,1:T(8,128)(2,1)S(1)}, bf16[512,256]{0,1:T(8,128)(2,1)}, u32[]{:S(2)}, u32[]{:S(2)}) collective-permute-start(bf16[512,256]{0,1:T(8,128)(2,1)S(1)} %broadcast_select_fusion.1), channel_id=1, source_target_pairs={{0,4},{4,8},{8,12},{12,16},{16,20},{20,24},{24,28},{28,32},{32,36}... | collective-permute-start | bytes 786440 | tf_op jit(solution)/shard_map/ppermute | solution.py:13
  63.5 6.7 %collective-permute-done = bf16[512,256]{0,1:T(8,128)(2,1)S(1)} collective-permute-done((bf16[512,256]{0,1:T(8,128)(2,1)S(1)}, bf16[512,256]{0,1:T(8,128)(2,1)S(1)}, u32[]{:S(2)}, u32[]{:S(2)}) %collective-permute-start) | collective-permute-done | bytes 262176 | tf_op jit(solution)/shard_map/ppermute | solution.py:13
  71.0 1.9 %collective-permute-start.1 = (bf16[512,256]{0,1:T(8,128)(2,1)}, bf16[512,256]{0,1:T(8,128)(2,1)}, u32[]{:S(2)}, u32[]{:S(2)}) collective-permute-start(bf16[512,256]{0,1:T(8,128)(2,1)} %broadcast_select_fusion.3), channel_id=1, source_target_pairs={{0,4},{4,8},{8,12},{12,16},{16,20},{20,24},{24,28},{28,32},{32,36}... | collective-permute-start | bytes 786440 | tf_op jit(solution)/shard_map/ppermute | solution.py:13
  72.9 1.3 maximum_convert_fusion
  74.2 0.9 copy.49
  75.1 1.1 concatenate.29
  76.3 0.8 concatenate.34
  77.5 1.0 broadcast_select_fusion
  78.5 6.2 %collective-permute-done.1 = bf16[512,256]{0,1:T(8,128)(2,1)} collective-permute-done((bf16[512,256]{0,1:T(8,128)(2,1)}, bf16[512,256]{0,1:T(8,128)(2,1)}, u32[]{:S(2)}, u32[]{:S(2)}) %collective-permute-start.1) | collective-permute-done | bytes 262176 | tf_op jit(solution)/shard_map/ppermute | solution.py:13
  84.7 1.0 broadcast_select_fusion.2
  85.7 2.2 %maximum_bitcast_fusion = (bf16[4,1536,64]{1,2,0:T(8,128)(2,1)S(1)}, bf16[4,1536,64]{1,2,0:T(8,128)(2,1)}) fusion(bf16[512,4,64]{0,2,1:T(8,128)(2,1)S(1)} %concatenate.29, bf16[512,4,64]{0,2,1:T(8,128)(2,1)} %bitcast.6, bf16[512,4,64]{0,2,1:T(8,128)(2,1)S(1)} %bitcast.95, bf16[512,4,64]{0,2,1:T(8,128)(2,1)} %concatenate.34, bf16[512,4,64]{0,2,1:T(8,128)(2,1)} %bitcast.93, ...), kind=kLoop, calls=%fused_computation.34 | loop fusion | flops 4718592 | bytes 3145728 | tf_op jit(solution)/shard_map/transpose | solution.py:98
  87.9 32.6 %while.14 = (s32[]{:T(128)}, bf16[4,512,64]{1,2,0:T(8,128)(2,1)}, bf16[4,512,64]{1,2,0:T(8,128)(2,1)S(1)}, bf16[4,1536,64]{1,2,0:T(8,128)(2,1)S(1)}, f32[4,64,64...) while((s32[]{:T(128)}, bf16[4,512,64]{1,2,0:T(8,128)(2,1)}, ...), condition=%wide.region_3.4_spmd.clone, body=%wide.region_2.3_spmd.clone.sunk | while | flops 839417856 | bytes 10323121 | solution.py:117
  89.1 4.8 %select_convert_fusion.2 = bf16[512,1536]{1,0:T(8,128)(2,1)S(1)} fusion(f32[512,1536]{1,0:T(8,128)S(1)} %convolution_multiply_fusion.2, f32[64,512]{1,0:T(8,128)S(1)} %fusion.81, s32[1536]{0:T(1024)S(1)} %get-tuple-element.296, pred[1536]{0:T(1024)(128)(4,1)S(1)} %get-tuple-element.297, pred[1536]{0:T(1024)(128)(4,1)S(1)} %copy-done.10, ...), kind=kOutput, calls=%fused_computation.6.clone.1 | convolution fusion | flops 612040704 | bytes 4865024 | tf_op jit(solution)/shard_map/while/body/eval_jaxpr/dot_general | solution.py:110
  93.9 2.2 %fusion.82 = bf16[4,512,64]{1,2,0:T(8,128)(2,1)} fusion(bf16[4,512,64]{1,2,0:T(8,128)(2,1)} %get-tuple-element.277, s32[]{:T(128)} %get-tuple-element.276, bf16[512,1536]{1,0:T(8,128)(2,1)S(1)} %select_convert_fusion.2, bf16[4,1536,64]{1,2,0:T(8,128)(2,1)} %get-tuple-element.293), kind=kOutput, calls=%fused_computation.11.clone.1 | convolution fusion | flops 100696064 | bytes 1836032 | tf_op jit(solution)/shard_map/while/body/eval_jaxpr/dot_general | solution.py:115
  97.2 4.8 %select_convert_fusion.2 = bf16[512,1536]{1,0:T(8,128)(2,1)S(1)} fusion(f32[512,1536]{1,0:T(8,128)S(1)} %convolution_multiply_fusion.2, f32[64,512]{1,0:T(8,128)S(1)} %fusion.81, s32[1536]{0:T(1024)S(1)} %get-tuple-element.296, pred[1536]{0:T(1024)(128)(4,1)S(1)} %get-tuple-element.297, pred[1536]{0:T(1024)(128)(4,1)S(1)} %copy-done.10, ...), kind=kOutput, calls=%fused_computation.6.clone.1 | convolution fusion | flops 612040704 | bytes 4865024 | tf_op jit(solution)/shard_map/while/body/eval_jaxpr/dot_general | solution.py:110
  102.0 2.2 %fusion.82 = bf16[4,512,64]{1,2,0:T(8,128)(2,1)} fusion(bf16[4,512,64]{1,2,0:T(8,128)(2,1)} %get-tuple-element.277, s32[]{:T(128)} %get-tuple-element.276, bf16[512,1536]{1,0:T(8,128)(2,1)S(1)} %select_convert_fusion.2, bf16[4,1536,64]{1,2,0:T(8,128)(2,1)} %get-tuple-element.293), kind=kOutput, calls=%fused_computation.11.clone.1 | convolution fusion | flops 100696064 | bytes 1836032 | tf_op jit(solution)/shard_map/while/body/eval_jaxpr/dot_general | solution.py:115
  105.3 4.8 %select_convert_fusion.2 = bf16[512,1536]{1,0:T(8,128)(2,1)S(1)} fusion(f32[512,1536]{1,0:T(8,128)S(1)} %convolution_multiply_fusion.2, f32[64,512]{1,0:T(8,128)S(1)} %fusion.81, s32[1536]{0:T(1024)S(1)} %get-tuple-element.296, pred[1536]{0:T(1024)(128)(4,1)S(1)} %get-tuple-element.297, pred[1536]{0:T(1024)(128)(4,1)S(1)} %copy-done.10, ...), kind=kOutput, calls=%fused_computation.6.clone.1 | convolution fusion | flops 612040704 | bytes 4865024 | tf_op jit(solution)/shard_map/while/body/eval_jaxpr/dot_general | solution.py:110
  110.1 2.2 %fusion.82 = bf16[4,512,64]{1,2,0:T(8,128)(2,1)} fusion(bf16[4,512,64]{1,2,0:T(8,128)(2,1)} %get-tuple-element.277, s32[]{:T(128)} %get-tuple-element.276, bf16[512,1536]{1,0:T(8,128)(2,1)S(1)} %select_convert_fusion.2, bf16[4,1536,64]{1,2,0:T(8,128)(2,1)} %get-tuple-element.293), kind=kOutput, calls=%fused_computation.11.clone.1 | convolution fusion | flops 100696064 | bytes 1836032 | tf_op jit(solution)/shard_map/while/body/eval_jaxpr/dot_general | solution.py:115
  113.5 4.8 %select_convert_fusion.2 = bf16[512,1536]{1,0:T(8,128)(2,1)S(1)} fusion(f32[512,1536]{1,0:T(8,128)S(1)} %convolution_multiply_fusion.2, f32[64,512]{1,0:T(8,128)S(1)} %fusion.81, s32[1536]{0:T(1024)S(1)} %get-tuple-element.296, pred[1536]{0:T(1024)(128)(4,1)S(1)} %get-tuple-element.297, pred[1536]{0:T(1024)(128)(4,1)S(1)} %copy-done.10, ...), kind=kOutput, calls=%fused_computation.6.clone.1 | convolution fusion | flops 612040704 | bytes 4865024 | tf_op jit(solution)/shard_map/while/body/eval_jaxpr/dot_general | solution.py:110
  118.3 2.2 %fusion.82 = bf16[4,512,64]{1,2,0:T(8,128)(2,1)} fusion(bf16[4,512,64]{1,2,0:T(8,128)(2,1)} %get-tuple-element.277, s32[]{:T(128)} %get-tuple-element.276, bf16[512,1536]{1,0:T(8,128)(2,1)S(1)} %select_convert_fusion.2, bf16[4,1536,64]{1,2,0:T(8,128)(2,1)} %get-tuple-element.293), kind=kOutput, calls=%fused_computation.11.clone.1 | convolution fusion | flops 100696064 | bytes 1836032 | tf_op jit(solution)/shard_map/while/body/eval_jaxpr/dot_general | solution.py:115
  120.4 1.1 all_to_all.61
  121.7 11.4 %all_to_all.67 = bf16[4,128,256]{2,1,0:T(8,128)(2,1)S(1)} all-to-all(bf16[4,128,256]{2,1,0:T(8,128)(2,1)S(1)} %copy.60), channel_id=1, replica_groups=mesh['wide'=192,'narrow'=4] {'narrow'}, dimensions={0} | all-to-all | bytes 524288 | tf_op jit(solution)/shard_map/all_to_all | solution.py:119
  133.5 2.1 %fusion.24 = bf16[128,1024]{1,0:T(8,128)(2,1)} fusion(bf16[1024,1024]{1,0:T(8,128)(2,1)S(1)} %copy-done, bf16[128,1024]{1,0:T(8,128)(2,1)S(1)} %copy-done.1, f32[128,1024]{1,0:T(8,128)S(1)} %bitcast.90, bf16[128,4096]{1,0:T(8,128)(2,1)} %copy-done.2, f32[128]{0:T(128)S(1)} %add_rsqrt_fusion, f32[128]{0:T(128)S(1)} %broadcast_multiply_fusion), kind=kOutput, calls=%fused_computation.32 | convolution fusion | flops 269484032 | bytes 3408896 | tf_op jit(solution)/shard_map/dot_general | solution.py:123
  (74 shorter events, 10.5 us)
Async XLA Ops:
  0.0 133.5 %copy-start = (bf16[1024,1024]{1,0:T(8,128)(2,1)S(1)}, bf16[1024,1024]{1,0:T(8,128)(2,1)}, u32[]{:S(2)}) copy-start(bf16[1024,1024]{1,0:T(8,128)(2,1)} %param.18) | copy-start | bytes 6291460
  7.3 1.0 copy-start.2
  8.3 5.2 %copy-start.6 = (s32[512]{0:T(512)S(1)}, s32[512]{0:T(512)}, u32[]{:S(2)}) copy-start(s32[512]{0:T(512)} %param.12) | copy-start | bytes 6148
  8.3 8.9 %copy-start.5 = (bf16[1024,256]{1,0:T(8,128)(2,1)S(1)}, bf16[1024,256]{1,0:T(8,128)(2,1)}, u32[]{:S(2)}) copy-start(bf16[1024,256]{1,0:T(8,128)(2,1)} %param.15) | copy-start | bytes 1572868
  8.3 10.8 %copy-start.8 = (s32[192]{0:T(256)S(1)}, s32[192]{0:T(256)}, u32[]{:S(2)}) copy-start(s32[192]{0:T(256)} %param.13) | copy-start | bytes 2308
  9.2 29.8 %all-to-all-start.2 = ((bf16[128,4,256]{0,2,1:T(8,128)(2,1)}), bf16[128,4,256]{0,2,1:T(8,128)(2,1)S(1)}, u32[]{:S(2)}, u32[]{:S(2)}) async-start(bf16[128,4,256]{0,2,1:T(8,128)(2,1)} %bitcast.9), calls=%async_computation.2 | async-start | bytes 524288 | tf_op jit(solution)/shard_map/all_to_all | solution.py:48
  14.0 19.4 %collective-permute-start.2 = (bf16[512]{0:T(512)(128)(2,1)}, bf16[512]{0:T(512)(128)(2,1)}, u32[]{:S(2)}, u32[]{:S(2)}) collective-permute-start(bf16[512]{0:T(512)(128)(2,1)} %convert_element_type.64), channel_id=1, source_target_pairs={{0,4},{4,8},{8,12},{12,16},{16,20},{20,24},{24,28},{28,32},{32,36}... | collective-permute-start | bytes 3080 | tf_op jit(solution)/shard_map/ppermute | solution.py:13
  31.0 39.2 %copy-start.4 = (bf16[512,256]{0,1:T(8,128)(2,1)S(1)}, bf16[512,256]{0,1:T(8,128)(2,1)}, u32[]{:S(2)}) copy-start(bf16[512,256]{0,1:T(8,128)(2,1)} %copy.70) | copy-start | bytes 786436
  34.7 22.6 %collective-permute-start.3 = (bf16[512]{0:T(512)(128)(2,1)}, bf16[512]{0:T(512)(128)(2,1)}, u32[]{:S(2)}, u32[]{:S(2)}) collective-permute-start(bf16[512]{0:T(512)(128)(2,1)} %slice_select_fusion), channel_id=1, source_target_pairs={{0,4},{4,8},{8,12},{12,16},{16,20},{20,24},{24,28},{28,32},{32,36}... | collective-permute-start | bytes 3080 | tf_op jit(solution)/shard_map/ppermute | solution.py:13
  39.0 12.5 %all-to-all-start.1 = ((bf16[128,4,256]{0,2,1:T(8,128)(2,1)}), bf16[128,4,256]{0,2,1:T(8,128)(2,1)S(1)}, u32[]{:S(2)}, u32[]{:S(2)}) async-start(bf16[128,4,256]{0,2,1:T(8,128)(2,1)} %bitcast.3), calls=%async_computation.1 | async-start | bytes 524288 | tf_op jit(solution)/shard_map/all_to_all | solution.py:47
  43.9 15.0 %collective-permute-start.4 = (bf16[512,256]{0,1:T(8,128)(2,1)S(1)}, bf16[512,256]{0,1:T(8,128)(2,1)}, u32[]{:S(2)}, u32[]{:S(2)}) collective-permute-start(bf16[512,256]{0,1:T(8,128)(2,1)S(1)} %copy_bitcast_fusion), channel_id=1, source_target_pairs={{0,4},{4,8},{8,12},{12,16},{16,20},{20,24},{24,28},{28,32},{32,36}... | collective-permute-start | bytes 786440 | tf_op jit(solution)/shard_map/ppermute | solution.py:13
  51.5 25.6 %all-to-all-start = ((bf16[128,4,256]{0,2,1:T(8,128)(2,1)}), bf16[128,4,256]{0,2,1:T(8,128)(2,1)S(1)}, u32[]{:S(2)}, u32[]{:S(2)}) async-start(bf16[128,4,256]{0,2,1:T(8,128)(2,1)} %bitcast), calls=%async_computation | async-start | bytes 524288 | tf_op jit(solution)/shard_map/all_to_all | solution.py:46
  55.0 15.3 %collective-permute-start = (bf16[512,256]{0,1:T(8,128)(2,1)S(1)}, bf16[512,256]{0,1:T(8,128)(2,1)S(1)}, u32[]{:S(2)}, u32[]{:S(2)}) collective-permute-start(bf16[512,256]{0,1:T(8,128)(2,1)S(1)} %copy_bitcast_fusion.1), channel_id=1, source_target_pairs={{0,4},{4,8},{8,12},{12,16},{16,20},{20,24},{24,28},{28,32},{32,36}... | collective-permute-start | bytes 786440 | tf_op jit(solution)/shard_map/ppermute | solution.py:13
  59.9 18.6 %copy-start.3 = (bf16[512,256]{0,1:T(8,128)(2,1)}, bf16[512,256]{0,1:T(8,128)(2,1)S(1)}, u32[]{:S(2)}) copy-start(bf16[512,256]{0,1:T(8,128)(2,1)S(1)} %broadcast_select_fusion.1) | copy-start | bytes 786436
  59.9 17.6 %collective-permute-start.5 = (bf16[512,256]{0,1:T(8,128)(2,1)S(1)}, bf16[512,256]{0,1:T(8,128)(2,1)}, u32[]{:S(2)}, u32[]{:S(2)}) collective-permute-start(bf16[512,256]{0,1:T(8,128)(2,1)S(1)} %broadcast_select_fusion.1), channel_id=1, source_target_pairs={{0,4},{4,8},{8,12},{12,16},{16,20},{20,24},{24,28},{28,32},{32,36}... | collective-permute-start | bytes 786440 | tf_op jit(solution)/shard_map/ppermute | solution.py:13
  71.0 13.7 %collective-permute-start.1 = (bf16[512,256]{0,1:T(8,128)(2,1)}, bf16[512,256]{0,1:T(8,128)(2,1)}, u32[]{:S(2)}, u32[]{:S(2)}) collective-permute-start(bf16[512,256]{0,1:T(8,128)(2,1)} %broadcast_select_fusion.3), channel_id=1, source_target_pairs={{0,4},{4,8},{8,12},{12,16},{16,20},{20,24},{24,28},{28,32},{32,36}... | collective-permute-start | bytes 786440 | tf_op jit(solution)/shard_map/ppermute | solution.py:13
  78.5 9.4 %copy-start.9 = (pred[1536]{0:T(1024)(128)(4,1)S(1)}, pred[1536]{0:T(1024)(128)(4,1)}, u32[]{:S(2)}) copy-start(pred[1536]{0:T(1024)(128)(4,1)} %get-tuple-element.273) | copy-start | bytes 4612
  87.9 1.2 copy-start.7
  87.9 1.2 copy-start.10
  96.0 1.2 copy-start.7
  96.0 1.2 copy-start.10
  104.2 1.2 copy-start.7
  104.2 1.2 copy-start.10
  112.3 1.2 copy-start.7
  112.3 1.2 copy-start.10
  120.4 13.1 %copy-start.1 = (bf16[128,1024]{1,0:T(8,128)(2,1)S(1)}, bf16[128,1024]{1,0:T(8,128)(2,1)}, u32[]{:S(2)}) copy-start(bf16[128,1024]{1,0:T(8,128)(2,1)} %param.11) | copy-start | bytes 786436
where the time goes:
time: 137 us; the launch traced here: 136 us
  matrix products  42.8 us (31%)
  starting transfers between devices  29.7 us (22%)
  waiting for transfers between devices  19 us (14%)
  local copies, waits for them, and re-layouts  16.2 us (12%)
  other arithmetic  14.4 us (11%)
  blocking collectives  11.4 us (8%)
  between operations  2.1 us (2%)
    dot_general x4, matrix products, one_head(): lax.dot_general(query_bias, key_hot, (((1,), (1,)), ((), ())), precision=...  19.2 us
    ppermute x6, starting transfers between devices, passed_along(): return lax.ppermute(block, axis, route)  17.2 us
    ppermute x6, waiting for transfers between devices, passed_along(): return lax.ppermute(block, axis, route)  13.8 us
    all_to_all x1, blocking collectives, per_device(): lax.all_to_all(attended, 'narrow', split_axis=0, concat_axis=1, tiled=True)  11.4 us
    dot_general x4, matrix products, one_head(): jnp.dot(weight, value_head, preferred_element_type=jnp.float32)  8.65 us
    unnamed x22, local copies, waits for them, and re-layouts  6.28 us
    all_to_all x1, waiting for transfers between devices, per_device(): lax.all_to_all(keys, 'narrow', split_axis=1, concat_axis=0, tiled=True)  5.14 us
    dot_general x1, matrix products, per_device(): jnp.dot(normed, w_input, preferred_element_type=jnp.float32)  4.89 us
  transfers between devices with their start and end apart: 9, of which 4 were waited for; matrix products, arithmetic and copies ran while one was open for 18% of the time, Pallas kernels for 0%

commit v1 on v0

v1 whole, which is shorter than its diff:
```python
import jax
import jax.numpy as jnp
from jax import lax
from jax.experimental import pallas as pl
from jax.experimental.pallas import tpu as pltpu
from jax.sharding import Mesh, PartitionSpec as P


F32 = jnp.float32
BF16 = jnp.bfloat16
RING = ("side", "narrow")
ROWS = 128
LANES = 128
EXT = 136
NB = 64


def vmem():
    return pl.BlockSpec(memory_space=pltpu.VMEM)


def hbm():
    return pl.BlockSpec(memory_space=pltpu.HBM)


def limited(mib):
    return pltpu.CompilerParams(vmem_limit_bytes=mib << 20)


def cost(flops, moved):
    return pl.CostEstimate(flops=flops, bytes_accessed=moved, transcendentals=0)


def started(*copies):
    for copy in copies:
        copy.start()
    return copies


def silu_of_half(half):
    return half + half * jnp.tanh(half)


def standardised(values):
    mean = jnp.mean(values, axis=-1, keepdims=True)
    centred = values - mean
    var = jnp.mean(centred * centred, axis=-1, keepdims=True)
    return centred * lax.rsqrt(var + 1e-05)


STARTS = {"u": 0, "v": 1024, "q": 2048, "k": 3072}
ALL = 67_000_000


def weight_copies(w_hbm, ws, sems, kinds):
    width = ws.shape[2]
    return [
        pltpu.make_async_copy(w_hbm.at[:, pl.ds(STARTS[kind], width)], ws.at[i], sems.at[i])
        for i, kind in enumerate(kinds)
    ]


def place_parts(part, kind, n, place, valid, out_ref):
    lanes = slice(place * LANES, (place + 1) * LANES)
    if kind == "q":
        part = part * 0.0625
    if kind == "v":
        part = jnp.where(valid, part, 0.0)
    part = part.astype(BF16)
    out_ref[n, 0:ROWS, lanes] = part[:, 0:LANES]
    out_ref[4 + n, 0:ROWS, lanes] = part[:, LANES:]


def valid_rows(lag, counts):
    block = 2 * (lax.axis_index("outer") - lag) + lax.axis_index("side")
    count = counts[jnp.maximum(block, 0)]
    at = lax.broadcasted_iota(jnp.int32, (ROWS, 2 * LANES), 0)
    return at + lax.axis_index("narrow") * ROWS < count


def tail_rows(x_ref, out_ref):
    tail = x_ref[ROWS:EXT, 0 : out_ref.shape[2]]
    for s in range(8):
        out_ref[s, ROWS:EXT, :] = tail


def project_kernel(
    events_hbm, buckets_hbm, counts_hbm, w_hbm, normed_hbm, out_hbm, gate_hbm,
    events, buckets, counts, ws, normed, out, gate, in_sems, w_sems, out_sems
):
    small = started(
        pltpu.make_async_copy(events_hbm, events, in_sems.at[0]),
        pltpu.make_async_copy(buckets_hbm, buckets, in_sems.at[1]),
        pltpu.make_async_copy(counts_hbm, counts, in_sems.at[2]),
    )
    weights = started(*weight_copies(w_hbm, ws, w_sems, "qkvu"))
    for copy in small:
        copy.wait()
    x = standardised(events[...].astype(F32)).astype(BF16)
    normed[0:ROWS, :] = x
    own = buckets[pl.ds(lax.axis_index("narrow"), 1), :].astype(F32)
    width = normed.shape[1]
    row = jnp.concatenate([own] * (width // LANES), axis=1)
    normed[ROWS:EXT, :] = jnp.broadcast_to(row, (EXT - ROWS, width)).astype(BF16)
    sends = [pltpu.make_async_copy(normed, normed_hbm, out_sems.at[2])]
    sends[0].start()
    tail_rows(normed, out)
    valid = valid_rows(0, counts)
    for place, kind in enumerate("qkvu"):
        weights[place].wait()
        for n in range(4):
            lanes = slice(n * 2 * LANES, (n + 1) * 2 * LANES)
            w = ws[place, :, lanes]
            part = silu_of_half(0.5 * jnp.dot(x, w, preferred_element_type=F32))
            if kind == "u":
                gate[:, lanes] = part.astype(BF16)
            else:
                place_parts(part, kind, n, place, valid, out)
        if kind == "v":
            sends += started(pltpu.make_async_copy(out, out_hbm, out_sems.at[0]))
    sends += started(pltpu.make_async_copy(gate, gate_hbm, out_sems.at[1]))
    for copy in sends:
        copy.wait()


def project_call(events, buckets, counts, w_input):
    depth, width = w_input.shape
    return pl.pallas_call(
        project_kernel,
        out_shape=(
            jax.ShapeDtypeStruct((EXT, depth), BF16),
            jax.ShapeDtypeStruct((8, EXT, 3 * LANES), BF16),
            jax.ShapeDtypeStruct((ROWS, depth), BF16),
        ),
        in_specs=[hbm()] * 4,
        out_specs=(hbm(), hbm(), hbm()),
        scratch_shapes=[
            pltpu.VMEM((ROWS, depth), BF16),
            pltpu.VMEM((4, LANES), jnp.int32),
            pltpu.SMEM(counts.shape, jnp.int32),
            pltpu.VMEM((4, depth, 8 * LANES), BF16),
            pltpu.VMEM((EXT, depth), BF16),
            pltpu.VMEM((8, EXT, 3 * LANES), BF16),
            pltpu.VMEM((ROWS, depth), BF16),
            pltpu.SemaphoreType.DMA((3,)),
            pltpu.SemaphoreType.DMA((4,)),
            pltpu.SemaphoreType.DMA((3,)),
        ],
        cost_estimate=cost(2 * ROWS * depth * width, 2 * depth * width),
        compiler_params=pltpu.CompilerParams(vmem_limit_bytes=ALL),
        name="project_own",
    )(events, buckets, counts, w_input)


def project_prev_kernel(
    counts_hbm, x_hbm, w_hbm, out_hbm, counts, x, ws, out, in_sems, w_sems, out_sem
):
    small = started(
        pltpu.make_async_copy(x_hbm, x, in_sems.at[0]),
        pltpu.make_async_copy(counts_hbm, counts, in_sems.at[1]),
    )
    weights = started(*weight_copies(w_hbm, ws, w_sems, "kv"))
    for copy in small:
        copy.wait()
    valid = valid_rows(1, counts)
    tail_rows(x, out)
    for place, kind in enumerate("kv"):
        weights[place].wait()
        for n in range(4):
            w = ws[place, :, n * 2 * LANES : (n + 1) * 2 * LANES]
            dot = jnp.dot(x[0:ROWS, :], w, preferred_element_type=F32)
            place_parts(silu_of_half(0.5 * dot), kind, n, place, valid, out)
    send = pltpu.make_async_copy(out, out_hbm, out_sem)
    send.start()
    send.wait()


def project_prev_call(normed, counts, w_input):
    depth = w_input.shape[0]
    return pl.pallas_call(
        project_prev_kernel,
        out_shape=jax.ShapeDtypeStruct((8, EXT, 2 * LANES), BF16),
        in_specs=[hbm()] * 3,
        out_specs=hbm(),
        scratch_shapes=[
            pltpu.SMEM(counts.shape, jnp.int32),
            pltpu.VMEM((EXT, depth), BF16),
            pltpu.VMEM((2, depth, 8 * LANES), BF16),
            pltpu.VMEM((8, EXT, 2 * LANES), BF16),
            pltpu.SemaphoreType.DMA((2,)),
            pltpu.SemaphoreType.DMA((2,)),
            pltpu.SemaphoreType.DMA,
        ],
        cost_estimate=cost(4 * ROWS * depth * depth, 4 * depth * depth),
        compiler_params=pltpu.CompilerParams(vmem_limit_bytes=ALL),
        name="project_prev",
    )(counts, normed, w_input)


def hot_of(row):
    column = jnp.transpose(jnp.broadcast_to(row, (LANES, LANES)))
    lane = lax.broadcasted_iota(jnp.int32, (LANES, LANES), 1)
    wanted = jnp.where(lane >= NB, lane - NB, lane).astype(F32)
    return jnp.where(column == wanted, 1.0, 0.0).astype(BF16)


def bias_rows(bias_ref):
    at = lax.broadcasted_iota(jnp.int32, (NB, LANES), 1)
    gap = jnp.where(at <= NB, at, LANES - at)
    step = lax.broadcasted_iota(jnp.int32, (NB, LANES), 0)
    pick = jnp.where(gap == step, 1.0, 0.0).astype(F32)
    return 0.5 * lax.dot_general(
        bias_ref[...],
        pick,
        (((1,), (0,)), ((), ())),
        precision=lax.Precision.HIGHEST,
        preferred_element_type=F32,
    )


def pair_table(rows, head):
    at = lax.broadcasted_iota(jnp.int32, rows.shape, 0)
    row = jnp.sum(jnp.where(at == head, rows, 0.0), axis=0, keepdims=True)
    whole = jnp.broadcast_to(row, (NB, LANES))
    first = pltpu.roll(whole, 0, 1, stride=1, stride_axis=0)
    second = pltpu.roll(whole, NB, 1, stride=1, stride_axis=0)
    lane = lax.broadcasted_iota(jnp.int32, (NB, LANES), 1)
    coarse = first.astype(BF16)
    fine = (second - second.astype(BF16).astype(F32)).astype(BF16)
    table = jnp.where(lane < NB, coarse.astype(F32), fine.astype(F32))
    return jnp.concatenate([table, jnp.zeros_like(table)], axis=0).astype(BF16)


TILE = 256


def part_of(ref, start, size, place):
    s, n = start // LANES, size // LANES
    lanes = slice(place * LANES, (place + 1) * LANES)
    return ref[s : s + n, 0:ROWS, lanes].reshape(size, LANES)


def attended_sum(left, key, key_hot, value, ends=None):
    right = jnp.concatenate([key, key_hot], axis=1)
    half = lax.dot_general(left, right, (((1,), (1,)), ((), ())), preferred_element_type=F32)
    weight = silu_of_half(half)
    if ends is not None:
        r = lax.broadcasted_iota(jnp.int32, weight.shape, 0) + ends
        c = lax.broadcasted_iota(jnp.int32, weight.shape, 1)
        weight = jnp.where(c <= r, weight, 0.0)
    return jnp.dot(weight.astype(BF16), value, preferred_element_type=F32)


def attend_own_kernel(own_ref, bias_ref, left_ref, sum_ref, hot):
    for s in range(8):
        at = slice(s * LANES, (s + 1) * LANES)
        hot[at, :] = hot_of(own_ref[s, ROWS : ROWS + 1, 0:LANES].astype(F32))
    rows = bias_rows(bias_ref)
    head = lax.axis_index("narrow") * 4 + lax.axis_index("side") * 2
    tables = [pair_table(rows, head + j) for j in range(2)]
    lane = lax.broadcasted_iota(jnp.int32, (TILE, LANES), 1)
    halves = [lane < NB, lane >= NB]
    for b in range(2):
        for t in range(2):
            start = b * 512 + t * TILE
            at = slice(start, start + TILE)
            query = part_of(own_ref, start, TILE, 0).astype(F32)
            spans = [(0, 512, None)] if b == 1 else []
            if t == 1:
                spans.append((b * 512, TILE, None))
            spans.append((start, TILE, 0))
            sums = []
            for j in range(2):
                shifts = jnp.dot(hot[at, :], tables[j], preferred_element_type=F32).astype(BF16)
                mine = jnp.where(halves[j], query, 0.0).astype(BF16)
                left = jnp.concatenate([mine, shifts], axis=1)
                left_ref[j, at, :] = left
                total = None
                for first, size, ends in spans:
                    part = attended_sum(
                        left,
                        part_of(own_ref, first, size, 1),
                        hot[first : first + size, :],
                        part_of(own_ref, first, size, 2),
                        ends,
                    )
                    total = part if total is None else total + part
                sums.append(total)
            sum_ref[at, :] = jnp.where(halves[0], sums[0], sums[1])


def attend_own_call(own, bias_rows_in):
    return pl.pallas_call(
        attend_own_kernel,
        out_shape=(
            jax.ShapeDtypeStruct((2, 1024, 2 * LANES), BF16),
            jax.ShapeDtypeStruct((1024, LANES), F32),
        ),
        in_specs=[vmem(), vmem()],
        out_specs=(vmem(), vmem()),
        scratch_shapes=[pltpu.VMEM((1024, LANES), BF16)],
        cost_estimate=cost(2 * 1024 * 1024 * 512, 4 << 20),
        compiler_params=pltpu.CompilerParams(vmem_limit_bytes=ALL),
        name="attend_own",
    )(own, bias_rows_in)


def attend_prev_kernel(
    left_hbm, sum_hbm, prev_hbm, cache_k, cache_v, cache_b, out_hbm,
    left_ref, sum_ref, prev_ref, out_ref, keys, values, rows, hot, sems, in_sems, out_sems
):
    first = lax.axis_index("outer") == 0
    prev_copy, left_copy, sum_copy = started(
        pltpu.make_async_copy(prev_hbm, prev_ref, in_sems.at[0]),
        pltpu.make_async_copy(left_hbm, left_ref, in_sems.at[1]),
        pltpu.make_async_copy(sum_hbm, sum_ref, in_sems.at[2]),
    )
    prev_copy.wait()

    @pl.when(first)
    def _():
        start = pl.multiple_of(lax.axis_index("side") * LANES, LANES)
        copies = started(
            pltpu.make_async_copy(cache_k.at[:, pl.ds(start, LANES)], keys, sems.at[0]),
            pltpu.make_async_copy(cache_v.at[:, pl.ds(start, LANES)], values, sems.at[1]),
            pltpu.make_async_copy(cache_b, rows, sems.at[2]),
        )
        for copy in copies:
            copy.wait()

    @pl.when(jnp.logical_not(first))
    def _():
        for s in range(8):
            at = slice(s * LANES, (s + 1) * LANES)
            rows[s : s + 1, :] = prev_ref[s, ROWS : ROWS + 1, 0:LANES].astype(F32).astype(jnp.int32)
            keys[at, :] = prev_ref[s, 0:ROWS, 0:LANES]
            values[at, :] = prev_ref[s, 0:ROWS, LANES : 2 * LANES]

    for s in range(8):
        at = slice(s * LANES, (s + 1) * LANES)
        hot[at, :] = hot_of(rows[s : s + 1, :].astype(F32))
    left_copy.wait()
    sum_copy.wait()
    lane = lax.broadcasted_iota(jnp.int32, (TILE, LANES), 1)
    sends = []
    for b in range(2):
        for t in range(2):
            start = b * 512 + t * TILE
            at = slice(start, start + TILE)
            sums = []
            for j in range(2):
                total = None
                for begin in (0, 512) if b == 0 else (512,):
                    span = slice(begin, begin + 512)
                    part = attended_sum(left_ref[j, at, :], keys[span, :], hot[span, :], values[span, :])
                    total = part if total is None else total + part
                sums.append(total)
            whole = sum_ref[at, :] + jnp.where(lane < NB, sums[0], sums[1])
            s = start // LANES
            out_ref[s : s + 2, :, :] = whole.astype(BF16).reshape(2, LANES, LANES)
            two = pl.ds(s, 2)
            sends += started(
                pltpu.make_async_copy(out_ref.at[two], out_hbm.at[two], out_sems.at[s // 2])
            )
    for copy in sends:
        copy.wait()


def attend_prev_call(left, partial, prev, prior_keys, prior_values, prior_buckets):
    return pl.pallas_call(
        attend_prev_kernel,
        out_shape=jax.ShapeDtypeStruct((8, ROWS, LANES), BF16),
        in_specs=[hbm()] * 6,
        out_specs=hbm(),
        scratch_shapes=[
            pltpu.VMEM(left.shape, BF16),
            pltpu.VMEM(partial.shape, F32),
            pltpu.VMEM(prev.shape, BF16),
            pltpu.VMEM((8, ROWS, LANES), BF16),
            pltpu.VMEM((1024, LANES), BF16),
            pltpu.VMEM((1024, LANES), BF16),
            pltpu.VMEM((8, LANES), jnp.int32),
            pltpu.VMEM((1024, LANES), BF16),
            pltpu.SemaphoreType.DMA((3,)),
            pltpu.SemaphoreType.DMA((3,)),
            pltpu.SemaphoreType.DMA((4,)),
        ],
        cost_estimate=cost(4 * 1024 * 1024 * 1024, 4 << 20),
        compiler_params=pltpu.CompilerParams(vmem_limit_bytes=61 << 20),
        name="attend_prev",
    )(left, partial, prev, prior_keys, prior_values, prior_buckets)


def mix_kernel(attended_ref, gate_ref, events_ref, w_ref, out_ref):
    parts = [attended_ref[(c % 2) * 4 + c // 2] for c in range(8)]
    whole = jnp.concatenate(parts, axis=1).astype(F32)
    gated = (standardised(whole) * gate_ref[...].astype(F32)).astype(BF16)
    mixed = events_ref[...].astype(F32) + jnp.dot(
        gated, w_ref[...], preferred_element_type=F32
    )
    out_ref[...] = mixed.astype(BF16)


def mix_call(attended, gate, events, w_output):
    return pl.pallas_call(
        mix_kernel,
        out_shape=jax.ShapeDtypeStruct(events.shape, BF16),
        in_specs=[vmem(), vmem(), vmem(), vmem()],
        out_specs=vmem(),
        cost_estimate=cost(2 << 27, 3 << 20),
        compiler_params=limited(8),
        name="mix",
    )(attended, gate, events, w_output)


def exchanged(parts):
    return lax.all_to_all(parts, RING, split_axis=0, concat_axis=0, tiled=True)


def per_device(
    events, buckets, counts, prior_keys, prior_values, prior_buckets, w_input, w_output, time_bias
):
    outer = lax.axis_size("outer")
    normed, sent, gate = project_call(events, buckets.reshape(4, LANES), counts, w_input)
    earlier = lax.ppermute(normed, "outer", [(i, i + 1) for i in range(outer - 1)])
    own = exchanged(sent)
    sent = project_prev_call(earlier, counts, w_input)
    prev = exchanged(sent)
    left, partial = attend_own_call(own, time_bias.T)
    attended = attend_prev_call(
        left, partial, prev, prior_keys, prior_values, prior_buckets.reshape(8, LANES)
    )
    attended = exchanged(attended)
    return mix_call(attended, gate, events, w_output)


def solution(mesh):
    rings = Mesh(
        mesh.devices.reshape(mesh.devices.shape[0] // 2, 2, mesh.devices.shape[1]),
        ("outer", "side", "narrow"),
    )
    placed = (
        P(("outer", "side", "narrow"), None),
        P(("outer", "side")),
        P(),
        P(None, "narrow"),
        P(None, "narrow"),
        P(),
        P(),
        P(),
        P(),
    )
    return jax.shard_map(
        per_device,
        mesh=rings,
        in_specs=placed,
        out_specs=P(("outer", "side", "narrow"), None),
        check_vma=False,
    )
```

time: 137 us -> 64.7 us (0.47)
  the two profiles are of different devices: /device:TPU:512 before, /device:TPU:1 now
where the time goes in v1:
time: 64.7 us; the launch traced here: 64.3 us
  starting transfers between devices  22.7 us (35%)
  Pallas kernels  20.8 us (32%)
  blocking collectives  11 us (17%)
  waiting for transfers between devices  9.8 us (15%)
    all_to_all x2, starting transfers between devices, exchanged(): return lax.all_to_all(parts, RING, split_axis=0, concat_axis=0, tiled=True)  20.7 us
    all_to_all x1, blocking collectives, exchanged(): return lax.all_to_all(parts, RING, split_axis=0, concat_axis=0, tiled=True)  11 us
    ppermute x1, waiting for transfers between devices, per_device(): lax.ppermute(normed, 'outer', [(i, i + 1) for i in range(outer - 1)])  5.74 us
    pallas_call x1, Pallas kernels, attend_prev_call(): pl.pallas_call(attend_prev_kernel, out_shape=jax.ShapeDtypeStruct((8, ROW...  5.63 us
    pallas_call x1, Pallas kernels, attend_own_call(): pl.pallas_call(attend_own_kernel, out_shape=(jax.ShapeDtypeStruct((2, 102...  5.16 us
    pallas_call x1, Pallas kernels, project_call(): pl.pallas_call(project_kernel, out_shape=(jax.ShapeDtypeStruct((EXT, dept...  5.01 us
    all_to_all x2, waiting for transfers between devices, exchanged(): return lax.all_to_all(parts, RING, split_axis=0, concat_axis=0, tiled=True)  4.05 us
    pallas_call x1, Pallas kernels, project_prev_call(): pl.pallas_call(project_prev_kernel, out_shape=jax.ShapeDtypeStruct((8, EX...  3.67 us
  transfers between devices with their start and end apart: 3, of which 2 were waited for; matrix products, arithmetic and copies ran while one was open for 0% of the time, Pallas kernels for 14%

profile of v1, /device:TPU:1, one launch (start us, length us, event | category | flops | bytes accessed | tf_op | source)
XLA Modules:
  0.0 64.3 jit_solution(6774766788208827222)
XLA Ops:
  0.0 5.0 %project_own.1 = (bf16[136,1024]{1,0:T(8,128)(2,1)}, bf16[8,136,384]{2,1,0:T(8,128)(2,1)}, bf16[128,1024]{1,0:T(8,128)(2,1)}) custom-call(bf16[128,1024]{1,0:T(8,128)(2,1)} %events_ref.1, s32[4,128]{1,0:T(4,128)} %bitcast.3, s32[192]{0:T(256)} %counts_hbm.3, bf16[1024,4096]{1,0:T(8,128)(2,1)} %w_hbm.3), custom_call_target="tpu_custom_call" | custom-call | flops 1073741824 | bytes 8388608 | tf_op jit(solution)/shard_map/project_own/pallas_call | solution.py:128
  5.0 14.6 %all-to-all-start = ((bf16[8,136,384]{2,1,0:T(8,128)(2,1)}), bf16[8,136,384]{2,1,0:T(8,128)(2,1)}, u32[]{:S(2)}, u32[]{:S(2)}) async-start(bf16[8,136,384]{2,1,0:T(8,128)(2,1)} %get-tuple-element.10), calls=%async_computation | async-start | bytes 1671168 | tf_op jit(solution)/shard_map/all_to_all | solution.py:417
  19.6 2.0 %collective-permute-start = (bf16[136,1024]{1,0:T(8,128)(2,1)}, bf16[136,1024]{1,0:T(8,128)(2,1)}, u32[]{:S(2)}, u32[]{:S(2)}) collective-permute-start(bf16[136,1024]{1,0:T(8,128)(2,1)} %get-tuple-element.13), channel_id=1, source_target_pairs={{0,8},{8,16},{16,24},{24,32},{32,40},{40,48},{48,56},{56,64},{64,7... | collective-permute-start | bytes 835592 | tf_op jit(solution)/shard_map/ppermute | solution.py:425
  21.6 5.7 %collective-permute-done.x_hbm = bf16[136,1024]{1,0:T(8,128)(2,1)} collective-permute-done((bf16[136,1024]{1,0:T(8,128)(2,1)}, bf16[136,1024]{1,0:T(8,128)(2,1)}, u32[]{:S(2)}, u32[]{:S(2)}) %collective-permute-start) | collective-permute-done | bytes 278560 | tf_op jit(solution)/shard_map/ppermute | solution.py:425
  27.3 3.7 %project_prev.1 = bf16[8,136,256]{2,1,0:T(8,128)(2,1)} custom-call(s32[192]{0:T(256)} %counts_hbm.3, bf16[136,1024]{1,0:T(8,128)(2,1)} %collective-permute-done.x_hbm, bf16[1024,4096]{1,0:T(8,128)(2,1)} %w_hbm.3), custom_call_target="tpu_custom_call" | custom-call | flops 536870912 | bytes 4194304 | tf_op jit(solution)/shard_map/project_prev/pallas_call | solution.py:180
  31.0 0.0 all-to-all-done.own_ref
  31.0 6.1 %all-to-all-start.1 = ((bf16[8,136,256]{2,1,0:T(8,128)(2,1)}), bf16[8,136,256]{2,1,0:T(8,128)(2,1)}, u32[]{:S(2)}, u32[]{:S(2)}) async-start(bf16[8,136,256]{2,1,0:T(8,128)(2,1)} %project_prev.1), calls=%async_computation.1 | async-start | bytes 1114112 | tf_op jit(solution)/shard_map/all_to_all | solution.py:417
  37.2 5.2 %attend_own.1 = (bf16[2,1024,256]{2,1,0:T(8,128)(2,1)}, f32[1024,128]{1,0:T(8,128)}) custom-call(bf16[8,136,384]{2,1,0:T(8,128)(2,1)} %all-to-all-done.own_ref, f32[16,64]{1,0:T(8,128)} %bitcast.4), custom_call_target="tpu_custom_call" | custom-call | flops 1073741824 | bytes 4194304 | tf_op jit(solution)/shard_map/attend_own/pallas_call | solution.py:293
  42.3 0.0 copy-start
  42.3 0.0 copy-start.1
  42.3 0.0 copy-start.2
  42.3 4.0 %all-to-all-done.1.prev_hbm = bf16[8,136,256]{2,1,0:T(8,128)(2,1)} async-done(((bf16[8,136,256]{2,1,0:T(8,128)(2,1)}), bf16[8,136,256]{2,1,0:T(8,128)(2,1)}, u32[]{:S(2)}, u32[]{:S(2)}) %all-to-all-start.1) | async-done | bytes 557088 | tf_op jit(solution)/shard_map/all_to_all | solution.py:417
  46.4 5.6 %attend_prev.1 = bf16[8,128,128]{2,1,0:T(8,128)(2,1)} custom-call(bf16[2,1024,256]{2,1,0:T(8,128)(2,1)} %get-tuple-element.11.left_hbm, f32[1024,128]{1,0:T(8,128)} %get-tuple-element.12.sum_hbm, bf16[8,136,256]{2,1,0:T(8,128)(2,1)} %all-to-all-done.1.prev_hbm, bf16[1024,256]{1,0:T(8,128)(2,1)} %cache_k.1, bf16[1024,256]{1,0:T(8,128)(2,1)} %cache_v.1, ...), custom_call_target="tpu_custom_call" | custom-call | flops 4294967296 | bytes 4194304 | tf_op jit(solution)/shard_map/attend_prev/pallas_call | solution.py:370
  52.0 11.0 %all_to_all.15.attended_ref = bf16[8,128,128]{2,1,0:T(8,128)(2,1)S(1)} all-to-all(bf16[8,128,128]{2,1,0:T(8,128)(2,1)} %attend_prev.1), channel_id=1, replica_groups=mesh['outer'=96,'side'=2,'narrow'=4] {'side','narrow'}, dimensions={0} | all-to-all | bytes 524288 | tf_op jit(solution)/shard_map/all_to_all | solution.py:417
  63.0 0.0 copy-done
  63.0 0.0 copy-done.1
  63.0 0.0 copy-done.2
  63.0 1.3 %mix.1 = bf16[128,1024]{1,0:T(8,128)(2,1)} custom-call(bf16[8,128,128]{2,1,0:T(8,128)(2,1)S(1)} %all_to_all.15.attended_ref, bf16[128,1024]{1,0:T(8,128)(2,1)S(1)} %copy-done.2, bf16[128,1024]{1,0:T(8,128)(2,1)S(1)} %copy-done.1, bf16[1024,1024]{1,0:T(8,128)(2,1)S(1)} %copy-done), custom_call_target="tpu_custom_call" | custom-call | flops 268435456 | bytes 3145728 | tf_op jit(solution)/shard_map/mix/pallas_call | solution.py:405
Async XLA Ops:
  5.0 26.0 %all-to-all-start = ((bf16[8,136,384]{2,1,0:T(8,128)(2,1)}), bf16[8,136,384]{2,1,0:T(8,128)(2,1)}, u32[]{:S(2)}, u32[]{:S(2)}) async-start(bf16[8,136,384]{2,1,0:T(8,128)(2,1)} %get-tuple-element.10), calls=%async_computation | async-start | bytes 1671168 | tf_op jit(solution)/shard_map/all_to_all | solution.py:417
  19.6 7.7 %collective-permute-start = (bf16[136,1024]{1,0:T(8,128)(2,1)}, bf16[136,1024]{1,0:T(8,128)(2,1)}, u32[]{:S(2)}, u32[]{:S(2)}) collective-permute-start(bf16[136,1024]{1,0:T(8,128)(2,1)} %get-tuple-element.13), channel_id=1, source_target_pairs={{0,8},{8,16},{16,24},{24,32},{32,40},{40,48},{48,56},{56,64},{64,7... | collective-permute-start | bytes 835592 | tf_op jit(solution)/shard_map/ppermute | solution.py:425
  31.0 15.3 %all-to-all-start.1 = ((bf16[8,136,256]{2,1,0:T(8,128)(2,1)}), bf16[8,136,256]{2,1,0:T(8,128)(2,1)}, u32[]{:S(2)}, u32[]{:S(2)}) async-start(bf16[8,136,256]{2,1,0:T(8,128)(2,1)} %project_prev.1), calls=%async_computation.1 | async-start | bytes 1114112 | tf_op jit(solution)/shard_map/all_to_all | solution.py:417
  42.3 20.6 %copy-start = (bf16[1024,1024]{1,0:T(8,128)(2,1)S(1)}, bf16[1024,1024]{1,0:T(8,128)(2,1)}, u32[]{:S(2)}) copy-start(bf16[1024,1024]{1,0:T(8,128)(2,1)} %w_ref.1) | copy-start | bytes 6291460
  42.3 20.6 %copy-start.1 = (bf16[128,1024]{1,0:T(8,128)(2,1)S(1)}, bf16[128,1024]{1,0:T(8,128)(2,1)}, u32[]{:S(2)}) copy-start(bf16[128,1024]{1,0:T(8,128)(2,1)} %events_ref.1) | copy-start | bytes 786436
  42.3 20.6 %copy-start.2 = (bf16[128,1024]{1,0:T(8,128)(2,1)S(1)}, bf16[128,1024]{1,0:T(8,128)(2,1)}, u32[]{:S(2)}) copy-start(bf16[128,1024]{1,0:T(8,128)(2,1)} %get-tuple-element.14.gate_ref) | copy-start | bytes 786436

commit v2 on v1

--- a/solution.py
+++ b/solution.py
@@ -85,15 +85,15 @@
 
 
 def project_kernel(
-    events_hbm, buckets_hbm, counts_hbm, w_hbm, normed_hbm, out_hbm, gate_hbm,
-    events, buckets, counts, ws, normed, out, gate, in_sems, w_sems, out_sems
+    events_hbm, buckets_hbm, counts_hbm, w_hbm, normed_hbm, out_hbm,
+    events, buckets, counts, ws, normed, out, in_sems, w_sems, out_sems
 ):
     small = started(
         pltpu.make_async_copy(events_hbm, events, in_sems.at[0]),
         pltpu.make_async_copy(buckets_hbm, buckets, in_sems.at[1]),
         pltpu.make_async_copy(counts_hbm, counts, in_sems.at[2]),
     )
-    weights = started(*weight_copies(w_hbm, ws, w_sems, "qkvu"))
+    weights = started(*weight_copies(w_hbm, ws, w_sems, "qkv"))
     for copy in small:
         copy.wait()
     x = standardised(events[...].astype(F32)).astype(BF16)
@@ -102,23 +102,20 @@
     width = normed.shape[1]
     row = jnp.concatenate([own] * (width // LANES), axis=1)
     normed[ROWS:EXT, :] = jnp.broadcast_to(row, (EXT - ROWS, width)).astype(BF16)
-    sends = [pltpu.make_async_copy(normed, normed_hbm, out_sems.at[2])]
+    sends = [pltpu.make_async_copy(normed, normed_hbm, out_sems.at[3])]
     sends[0].start()
     tail_rows(normed, out)
     valid = valid_rows(0, counts)
-    for place, kind in enumerate("qkvu"):
+    for place, kind in enumerate("qkv"):
         weights[place].wait()
         for n in range(4):
-            lanes = slice(n * 2 * LANES, (n + 1) * 2 * LANES)
-            w = ws[place, :, lanes]
+            w = ws[place, :, n * 2 * LANES : (n + 1) * 2 * LANES]
             part = silu_of_half(0.5 * jnp.dot(x, w, preferred_element_type=F32))
-            if kind == "u":
-                gate[:, lanes] = part.astype(BF16)
-            else:
-                place_parts(part, kind, n, place, valid, out)
-        if kind == "v":
-            sends += started(pltpu.make_async_copy(out, out_hbm, out_sems.at[0]))
-    sends += started(pltpu.make_async_copy(gate, gate_hbm, out_sems.at[1]))
+            place_parts(part, kind, n, place, valid, out)
+        lanes = pl.ds(place * LANES, LANES)
+        sends += started(
+            pltpu.make_async_copy(out.at[:, :, lanes], out_hbm.at[:, :, lanes], out_sems.at[place])
+        )
     for copy in sends:
         copy.wait()
 
@@ -130,21 +127,19 @@
         out_shape=(
             jax.ShapeDtypeStruct((EXT, depth), BF16),
             jax.ShapeDtypeStruct((8, EXT, 3 * LANES), BF16),
-            jax.ShapeDtypeStruct((ROWS, depth), BF16),
         ),
         in_specs=[hbm()] * 4,
-        out_specs=(hbm(), hbm(), hbm()),
+        out_specs=(hbm(), hbm()),
         scratch_shapes=[
             pltpu.VMEM((ROWS, depth), BF16),
             pltpu.VMEM((4, LANES), jnp.int32),
             pltpu.SMEM(counts.shape, jnp.int32),
-            pltpu.VMEM((4, depth, 8 * LANES), BF16),
+            pltpu.VMEM((3, depth, 8 * LANES), BF16),
             pltpu.VMEM((EXT, depth), BF16),
             pltpu.VMEM((8, EXT, 3 * LANES), BF16),
-            pltpu.VMEM((ROWS, depth), BF16),
+            pltpu.SemaphoreType.DMA((3,)),
             pltpu.SemaphoreType.DMA((3,)),
             pltpu.SemaphoreType.DMA((4,)),
-            pltpu.SemaphoreType.DMA((3,)),
         ],
         cost_estimate=cost(2 * ROWS * depth * width, 2 * depth * width),
         compiler_params=pltpu.CompilerParams(vmem_limit_bytes=ALL),
@@ -195,6 +190,37 @@
         compiler_params=pltpu.CompilerParams(vmem_limit_bytes=ALL),
         name="project_prev",
     )(counts, normed, w_input)
+
+
+def gate_kernel(x_hbm, w_hbm, out_ref, x, ws, sems):
+    copies = started(
+        pltpu.make_async_copy(x_hbm, x, sems.at[0]),
+        pltpu.make_async_copy(w_hbm.at[:, pl.ds(STARTS["u"], ws.shape[1])], ws, sems.at[1]),
+    )
+    for copy in copies:
+        copy.wait()
+    for n in range(4):
+        lanes = slice(n * 2 * LANES, (n + 1) * 2 * LANES)
+        half = 0.5 * jnp.dot(x[0:ROWS, :], ws[:, lanes], preferred_element_type=F32)
+        out_ref[:, lanes] = silu_of_half(half).astype(BF16)
+
+
+def gate_call(normed, w_input):
+    depth = w_input.shape[0]
+    return pl.pallas_call(
+        gate_kernel,
+        out_shape=jax.ShapeDtypeStruct((ROWS, depth), BF16),
+        in_specs=[hbm(), hbm()],
+        out_specs=vmem(),
+        scratch_shapes=[
+            pltpu.VMEM((EXT, depth), BF16),
+            pltpu.VMEM((depth, depth), BF16),
+            pltpu.SemaphoreType.DMA((2,)),
+        ],
+        cost_estimate=cost(2 * ROWS * depth * depth, 2 * depth * depth),
+        compiler_params=pltpu.CompilerParams(vmem_limit_bytes=ALL),
+        name="project_u",
+    )(normed, w_input)
 
 
 def hot_of(row):
@@ -421,9 +447,10 @@
     events, buckets, counts, prior_keys, prior_values, prior_buckets, w_input, w_output, time_bias
 ):
     outer = lax.axis_size("outer")
-    normed, sent, gate = project_call(events, buckets.reshape(4, LANES), counts, w_input)
+    normed, sent = project_call(events, buckets.reshape(4, LANES), counts, w_input)
     earlier = lax.ppermute(normed, "outer", [(i, i + 1) for i in range(outer - 1)])
     own = exchanged(sent)
+    gate = gate_call(normed, w_input)
     sent = project_prev_call(earlier, counts, w_input)
     prev = exchanged(sent)
     left, partial = attend_own_call(own, time_bias.T)

time: 64.7 us -> 69.5 us (1.074)
  blocking collectives: 11 us -> 0 us
  starting transfers between devices: 22.7 us -> 28 us
  waiting for transfers between devices: 9.8 us -> 13.3 us
  local copies, waits for them, and re-layouts: 0.01 us -> 3.49 us
  Pallas kernels: 20.8 us -> 24.1 us
    all_to_all x1 -> x0, blocking collectives: 11 us -> none  [exchanged(): return lax.all_to_all(parts, RING, split_axis=0, concat_axis=0, tiled=True)]
    all_to_all x2 -> x3, starting transfers between devices: 20.7 us -> 26 us  [exchanged(): return lax.all_to_all(parts, RING, split_axis=0, concat_axis=0, tiled=True)]
    all_to_all x2 -> x3, waiting for transfers between devices: 4.05 us -> 7.59 us  [exchanged(): return lax.all_to_all(parts, RING, split_axis=0, concat_axis=0, tiled=True)]
    unnamed x6, local copies, waits for them, and re-layouts: 0.01 us -> 3.49 us
    pallas_call x0 -> x1, Pallas kernels: none -> 2.88 us  [gate_call(): pl.pallas_call(gate_kernel, out_shape=jax.ShapeDtypeStruct((ROWS, depth),...]
    pallas_call x1, Pallas kernels: 1.34 us -> 2.28 us  [mix_call(): pl.pallas_call(mix_kernel, out_shape=jax.ShapeDtypeStruct(events.shape, B...]
  transfers between devices with their start and end apart: 3 -> 4, of which waited for: 2 -> 3; matrix products, arithmetic and copies ran while one was open for 0% -> 0% of each run, Pallas kernels for 14% -> 17%
where the time goes in v2:
time: 69.5 us; the launch traced here: 68.9 us
  starting transfers between devices  28 us (40%)
  Pallas kernels  24.1 us (35%)
  waiting for transfers between devices  13.3 us (19%)
  local copies, waits for them, and re-layouts  3.49 us (5%)
    all_to_all x3, starting transfers between devices, exchanged(): return lax.all_to_all(parts, RING, split_axis=0, concat_axis=0, tiled=True)  26 us
    all_to_all x3, waiting for transfers between devices, exchanged(): return lax.all_to_all(parts, RING, split_axis=0, concat_axis=0, tiled=True)  7.59 us
    ppermute x1, waiting for transfers between devices, per_device(): lax.ppermute(normed, 'outer', [(i, i + 1) for i in range(outer - 1)])  5.73 us
    pallas_call x1, Pallas kernels, attend_prev_call(): pl.pallas_call(attend_prev_kernel, out_shape=jax.ShapeDtypeStruct((8, ROW...  5.64 us
    pallas_call x1, Pallas kernels, attend_own_call(): pl.pallas_call(attend_own_kernel, out_shape=(jax.ShapeDtypeStruct((2, 102...  5.17 us
    pallas_call x1, Pallas kernels, project_call(): pl.pallas_call(project_kernel, out_shape=(jax.ShapeDtypeStruct((EXT, dept...  4.42 us
    pallas_call x1, Pallas kernels, project_prev_call(): pl.pallas_call(project_prev_kernel, out_shape=jax.ShapeDtypeStruct((8, EX...  3.68 us
    unnamed x6, local copies, waits for them, and re-layouts  3.49 us
  transfers between devices with their start and end apart: 4, of which 3 were waited for; matrix products, arithmetic and copies ran while one was open for 0% of the time, Pallas kernels for 17%

profile of v2, /device:TPU:1, one launch (start us, length us, event | category | flops | bytes accessed | tf_op | source)
XLA Modules:
  0.0 68.9 jit_solution(15888144397536620205)
XLA Ops:
  0.0 4.4 %project_own.1 = (bf16[136,1024]{1,0:T(8,128)(2,1)}, bf16[8,136,384]{2,1,0:T(8,128)(2,1)}) custom-call(bf16[128,1024]{1,0:T(8,128)(2,1)} %events_ref.1, s32[4,128]{1,0:T(4,128)} %bitcast.3, s32[192]{0:T(256)} %counts_hbm.3, bf16[1024,4096]{1,0:T(8,128)(2,1)} %w_hbm.5), custom_call_target="tpu_custom_call" | custom-call | flops 1073741824 | bytes 8388608 | tf_op jit(solution)/shard_map/project_own/pallas_call | solution.py:125
  4.4 14.6 %all-to-all-start = ((bf16[8,136,384]{2,1,0:T(8,128)(2,1)}), bf16[8,136,384]{2,1,0:T(8,128)(2,1)}, u32[]{:S(2)}, u32[]{:S(2)}) async-start(bf16[8,136,384]{2,1,0:T(8,128)(2,1)} %get-tuple-element.9), calls=%async_computation | async-start | bytes 1671168 | tf_op jit(solution)/shard_map/all_to_all | solution.py:443
  19.0 2.0 %collective-permute-start = (bf16[136,1024]{1,0:T(8,128)(2,1)}, bf16[136,1024]{1,0:T(8,128)(2,1)}, u32[]{:S(2)}, u32[]{:S(2)}) collective-permute-start(bf16[136,1024]{1,0:T(8,128)(2,1)} %get-tuple-element.12.x_hbm), channel_id=1, source_target_pairs={{0,8},{8,16},{16,24},{24,32},{32,40},{40,48},{48,56},{56,64},{64,7... | collective-permute-start | bytes 835592 | tf_op jit(solution)/shard_map/ppermute | solution.py:451
  21.0 5.7 %collective-permute-done.x_hbm = bf16[136,1024]{1,0:T(8,128)(2,1)} collective-permute-done((bf16[136,1024]{1,0:T(8,128)(2,1)}, bf16[136,1024]{1,0:T(8,128)(2,1)}, u32[]{:S(2)}, u32[]{:S(2)}) %collective-permute-start) | collective-permute-done | bytes 278560 | tf_op jit(solution)/shard_map/ppermute | solution.py:451
  26.7 3.7 %project_prev.1 = bf16[8,136,256]{2,1,0:T(8,128)(2,1)} custom-call(s32[192]{0:T(256)} %counts_hbm.3, bf16[136,1024]{1,0:T(8,128)(2,1)} %collective-permute-done.x_hbm, bf16[1024,4096]{1,0:T(8,128)(2,1)} %w_hbm.5), custom_call_target="tpu_custom_call" | custom-call | flops 536870912 | bytes 4194304 | tf_op jit(solution)/shard_map/project_prev/pallas_call | solution.py:175
  30.4 0.0 all-to-all-done.own_ref
  30.4 6.1 %all-to-all-start.1 = ((bf16[8,136,256]{2,1,0:T(8,128)(2,1)}), bf16[8,136,256]{2,1,0:T(8,128)(2,1)}, u32[]{:S(2)}, u32[]{:S(2)}) async-start(bf16[8,136,256]{2,1,0:T(8,128)(2,1)} %project_prev.1), calls=%async_computation.1 | async-start | bytes 1114112 | tf_op jit(solution)/shard_map/all_to_all | solution.py:443
  36.6 5.2 %attend_own.1 = (bf16[2,1024,256]{2,1,0:T(8,128)(2,1)}, f32[1024,128]{1,0:T(8,128)}) custom-call(bf16[8,136,384]{2,1,0:T(8,128)(2,1)} %all-to-all-done.own_ref, f32[16,64]{1,0:T(8,128)} %bitcast.4), custom_call_target="tpu_custom_call" | custom-call | flops 1073741824 | bytes 4194304 | tf_op jit(solution)/shard_map/attend_own/pallas_call | solution.py:319
  41.8 4.0 %all-to-all-done.1.prev_hbm = bf16[8,136,256]{2,1,0:T(8,128)(2,1)} async-done(((bf16[8,136,256]{2,1,0:T(8,128)(2,1)}), bf16[8,136,256]{2,1,0:T(8,128)(2,1)}, u32[]{:S(2)}, u32[]{:S(2)}) %all-to-all-start.1) | async-done | bytes 557088 | tf_op jit(solution)/shard_map/all_to_all | solution.py:443
  45.8 5.6 %attend_prev.1 = bf16[8,128,128]{2,1,0:T(8,128)(2,1)} custom-call(bf16[2,1024,256]{2,1,0:T(8,128)(2,1)} %get-tuple-element.10.left_hbm, f32[1024,128]{1,0:T(8,128)} %get-tuple-element.11.sum_hbm, bf16[8,136,256]{2,1,0:T(8,128)(2,1)} %all-to-all-done.1.prev_hbm, bf16[1024,256]{1,0:T(8,128)(2,1)} %cache_k.1, bf16[1024,256]{1,0:T(8,128)(2,1)} %cache_v.1, ...), custom_call_target="tpu_custom_call" | custom-call | flops 4294967296 | bytes 4194304 | tf_op jit(solution)/shard_map/attend_prev/pallas_call | solution.py:396
  51.4 5.3 %all-to-all-start.2 = ((bf16[8,128,128]{2,1,0:T(8,128)(2,1)}), bf16[8,128,128]{2,1,0:T(8,128)(2,1)}, u32[]{:S(2)}, u32[]{:S(2)}) async-start(bf16[8,128,128]{2,1,0:T(8,128)(2,1)} %attend_prev.1), calls=%async_computation.2 | async-start | bytes 524288 | tf_op jit(solution)/shard_map/all_to_all | solution.py:443
  56.7 2.9 %project_u.1.gate_ref = bf16[128,1024]{1,0:T(8,128)(2,1)} custom-call(bf16[136,1024]{1,0:T(8,128)(2,1)} %get-tuple-element.12.x_hbm, bf16[1024,4096]{1,0:T(8,128)(2,1)} %w_hbm.5), custom_call_target="tpu_custom_call" | custom-call | flops 268435456 | bytes 2097152 | tf_op jit(solution)/shard_map/project_u/pallas_call | solution.py:210
  59.6 3.6 %all-to-all-done.2.attended_ref = bf16[8,128,128]{2,1,0:T(8,128)(2,1)} async-done(((bf16[8,128,128]{2,1,0:T(8,128)(2,1)}), bf16[8,128,128]{2,1,0:T(8,128)(2,1)}, u32[]{:S(2)}, u32[]{:S(2)}) %all-to-all-start.2) | async-done | bytes 262176 | tf_op jit(solution)/shard_map/all_to_all | solution.py:443
  63.1 0.0 copy-start
  63.1 1.6 %copy-done = bf16[1024,1024]{1,0:T(8,128)(2,1)S(1)} copy-done((bf16[1024,1024]{1,0:T(8,128)(2,1)S(1)}, bf16[1024,1024]{1,0:T(8,128)(2,1)}, u32[]{:S(2)}) %copy-start) | copy-done | bytes 2097176
  64.7 0.0 copy-start.1
  64.7 0.9 %copy-done.1 = bf16[128,1024]{1,0:T(8,128)(2,1)S(1)} copy-done((bf16[128,1024]{1,0:T(8,128)(2,1)S(1)}, bf16[128,1024]{1,0:T(8,128)(2,1)}, u32[]{:S(2)}) %copy-start.1) | copy-done | bytes 262168
  65.7 0.0 copy-start.2
  65.7 0.9 %copy-done.2 = bf16[128,1024]{1,0:T(8,128)(2,1)S(1)} copy-done((bf16[128,1024]{1,0:T(8,128)(2,1)S(1)}, bf16[128,1024]{1,0:T(8,128)(2,1)}, u32[]{:S(2)}) %copy-start.2) | copy-done | bytes 262168
  66.6 2.3 %mix.1 = bf16[128,1024]{1,0:T(8,128)(2,1)} custom-call(bf16[8,128,128]{2,1,0:T(8,128)(2,1)} %all-to-all-done.2.attended_ref, bf16[128,1024]{1,0:T(8,128)(2,1)S(1)} %copy-done.2, bf16[128,1024]{1,0:T(8,128)(2,1)S(1)} %copy-done.1, bf16[1024,1024]{1,0:T(8,128)(2,1)S(1)} %copy-done), custom_call_target="tpu_custom_call" | custom-call | flops 268435456 | bytes 3145728 | tf_op jit(solution)/shard_map/mix/pallas_call | solution.py:431
Async XLA Ops:
  4.4 26.0 %all-to-all-start = ((bf16[8,136,384]{2,1,0:T(8,128)(2,1)}), bf16[8,136,384]{2,1,0:T(8,128)(2,1)}, u32[]{:S(2)}, u32[]{:S(2)}) async-start(bf16[8,136,384]{2,1,0:T(8,128)(2,1)} %get-tuple-element.9), calls=%async_computation | async-start | bytes 1671168 | tf_op jit(solution)/shard_map/all_to_all | solution.py:443
  19.0 7.7 %collective-permute-start = (bf16[136,1024]{1,0:T(8,128)(2,1)}, bf16[136,1024]{1,0:T(8,128)(2,1)}, u32[]{:S(2)}, u32[]{:S(2)}) collective-permute-start(bf16[136,1024]{1,0:T(8,128)(2,1)} %get-tuple-element.12.x_hbm), channel_id=1, source_target_pairs={{0,8},{8,16},{16,24},{24,32},{32,40},{40,48},{48,56},{56,64},{64,7... | collective-permute-start | bytes 835592 | tf_op jit(solution)/shard_map/ppermute | solution.py:451
  30.4 15.3 %all-to-all-start.1 = ((bf16[8,136,256]{2,1,0:T(8,128)(2,1)}), bf16[8,136,256]{2,1,0:T(8,128)(2,1)}, u32[]{:S(2)}, u32[]{:S(2)}) async-start(bf16[8,136,256]{2,1,0:T(8,128)(2,1)} %project_prev.1), calls=%async_computation.1 | async-start | bytes 1114112 | tf_op jit(solution)/shard_map/all_to_all | solution.py:443
  51.4 11.7 %all-to-all-start.2 = ((bf16[8,128,128]{2,1,0:T(8,128)(2,1)}), bf16[8,128,128]{2,1,0:T(8,128)(2,1)}, u32[]{:S(2)}, u32[]{:S(2)}) async-start(bf16[8,128,128]{2,1,0:T(8,128)(2,1)} %attend_prev.1), calls=%async_computation.2 | async-start | bytes 524288 | tf_op jit(solution)/shard_map/all_to_all | solution.py:443
  63.1 1.6 %copy-start = (bf16[1024,1024]{1,0:T(8,128)(2,1)S(1)}, bf16[1024,1024]{1,0:T(8,128)(2,1)}, u32[]{:S(2)}) copy-start(bf16[1024,1024]{1,0:T(8,128)(2,1)} %w_ref.1) | copy-start | bytes 6291460
  64.7 0.9 %copy-start.1 = (bf16[128,1024]{1,0:T(8,128)(2,1)S(1)}, bf16[128,1024]{1,0:T(8,128)(2,1)}, u32[]{:S(2)}) copy-start(bf16[128,1024]{1,0:T(8,128)(2,1)} %events_ref.1) | copy-start | bytes 786436
  65.7 0.9 %copy-start.2 = (bf16[128,1024]{1,0:T(8,128)(2,1)S(1)}, bf16[128,1024]{1,0:T(8,128)(2,1)}, u32[]{:S(2)}) copy-start(bf16[128,1024]{1,0:T(8,128)(2,1)} %project_u.1.gate_ref) | copy-start | bytes 786436

commit v3 on v2

--- a/solution.py
+++ b/solution.py
@@ -336,26 +336,35 @@
     left_ref, sum_ref, prev_ref, out_ref, keys, values, rows, hot, sems, in_sems, out_sems
 ):
     first = lax.axis_index("outer") == 0
-    prev_copy, left_copy, sum_copy = started(
-        pltpu.make_async_copy(prev_hbm, prev_ref, in_sems.at[0]),
+    lanes = pl.ds(pl.multiple_of(lax.axis_index("side") * LANES, LANES), LANES)
+    cached = (
+        pltpu.make_async_copy(cache_k.at[:, lanes], keys, sems.at[0]),
+        pltpu.make_async_copy(cache_v.at[:, lanes], values, sems.at[1]),
+        pltpu.make_async_copy(cache_b, rows, sems.at[2]),
+    )
+    prev_copy = pltpu.make_async_copy(prev_hbm, prev_ref, in_sems.at[0])
+
+    @pl.when(first)
+    def _():
+        started(*cached)
+
+    @pl.when(jnp.logical_not(first))
+    def _():
+        prev_copy.start()
+
+    left_copy, sum_copy = started(
         pltpu.make_async_copy(left_hbm, left_ref, in_sems.at[1]),
         pltpu.make_async_copy(sum_hbm, sum_ref, in_sems.at[2]),
     )
-    prev_copy.wait()
 
     @pl.when(first)
     def _():
-        start = pl.multiple_of(lax.axis_index("side") * LANES, LANES)
-        copies = started(
-            pltpu.make_async_copy(cache_k.at[:, pl.ds(start, LANES)], keys, sems.at[0]),
-            pltpu.make_async_copy(cache_v.at[:, pl.ds(start, LANES)], values, sems.at[1]),
-            pltpu.make_async_copy(cache_b, rows, sems.at[2]),
-        )
-        for copy in copies:
+        for copy in cached:
             copy.wait()
 
     @pl.when(jnp.logical_not(first))
     def _():
+        prev_copy.wait()
         for s in range(8):
             at = slice(s * LANES, (s + 1) * LANES)
             rows[s : s + 1, :] = prev_ref[s, ROWS : ROWS + 1, 0:LANES].astype(F32).astype(jnp.int32)
@@ -452,8 +461,19 @@
     own = exchanged(sent)
     gate = gate_call(normed, w_input)
     sent = project_prev_call(earlier, counts, w_input)
-    prev = exchanged(sent)
-    left, partial = attend_own_call(own, time_bias.T)
+
+    def cached(own, sent, bias):
+        left, partial = attend_own_call(own, bias)
+        return left, partial, sent
+
+    def received(own, sent, bias):
+        prev = exchanged(sent)
+        left, partial = attend_own_call(own, bias)
+        return left, partial, prev
+
+    left, partial, prev = lax.cond(
+        lax.axis_index("outer") == 0, cached, received, own, sent, time_bias.T
+    )
     attended = attend_prev_call(
         left, partial, prev, prior_keys, prior_values, prior_buckets.reshape(8, LANES)
     )

time: 69.5 us -> 67.9 us (0.977)
  the two profiles are of different devices: /device:TPU:1 before, /device:TPU:8 now
where the time goes in v3:
time: 67.9 us; the launch traced here: 67.4 us
  waiting for transfers between devices  24.3 us (36%)
  Pallas kernels  23.2 us (34%)
  starting transfers between devices  16.3 us (24%)
  local copies, waits for them, and re-layouts  3.49 us (5%)
    ppermute x1, waiting for transfers between devices, per_device(): lax.ppermute(normed, 'outer', [(i, i + 1) for i in range(outer - 1)])  14.7 us
    all_to_all x3, starting transfers between devices, exchanged(): return lax.all_to_all(parts, RING, split_axis=0, concat_axis=0, tiled=True)  12.8 us
    all_to_all x3, waiting for transfers between devices, exchanged(): return lax.all_to_all(parts, RING, split_axis=0, concat_axis=0, tiled=True)  9.66 us
    pallas_call x1, Pallas kernels, attend_own_call(): pl.pallas_call(attend_own_kernel, out_shape=(jax.ShapeDtypeStruct((2, 102...  5.16 us
    pallas_call x1, Pallas kernels, attend_prev_call(): pl.pallas_call(attend_prev_kernel, out_shape=jax.ShapeDtypeStruct((8, ROW...  4.75 us
    pallas_call x1, Pallas kernels, project_call(): pl.pallas_call(project_kernel, out_shape=(jax.ShapeDtypeStruct((EXT, dept...  4.42 us
    pallas_call x1, Pallas kernels, project_prev_call(): pl.pallas_call(project_prev_kernel, out_shape=jax.ShapeDtypeStruct((8, EX...  3.67 us
    unnamed x8, local copies, waits for them, and re-layouts  3.49 us
  transfers between devices with their start and end apart: 4, of which 3 were waited for; matrix products, arithmetic and copies ran while one was open for 0% of the time, Pallas kernels for 17%

profile of v3, /device:TPU:8, one launch (start us, length us, event | category | flops | bytes accessed | tf_op | source)
XLA Modules:
  0.0 67.4 jit_solution(11077773569131319983)
XLA Ops:
  0.0 0.0 copy-start.3
  0.0 4.4 %project_own.1 = (bf16[136,1024]{1,0:T(8,128)(2,1)}, bf16[8,136,384]{2,1,0:T(8,128)(2,1)}) custom-call(bf16[128,1024]{1,0:T(8,128)(2,1)} %events_ref.1, s32[4,128]{1,0:T(4,128)} %bitcast.3, s32[192]{0:T(256)} %counts_hbm.3, bf16[1024,4096]{1,0:T(8,128)(2,1)} %w_hbm.5), custom_call_target="tpu_custom_call" | custom-call | flops 1073741824 | bytes 8388608 | tf_op jit(solution)/shard_map/project_own/pallas_call | solution.py:125
  4.4 4.3 %all-to-all-start.1 = ((bf16[8,136,384]{2,1,0:T(8,128)(2,1)}), bf16[8,136,384]{2,1,0:T(8,128)(2,1)}, u32[]{:S(2)}, u32[]{:S(2)}) async-start(bf16[8,136,384]{2,1,0:T(8,128)(2,1)} %get-tuple-element.32), calls=%async_computation.1 | async-start | bytes 1671168 | tf_op jit(solution)/shard_map/all_to_all | solution.py:452
  8.7 3.5 %collective-permute-start = (bf16[136,1024]{1,0:T(8,128)(2,1)}, bf16[136,1024]{1,0:T(8,128)(2,1)}, u32[]{:S(2)}, u32[]{:S(2)}) collective-permute-start(bf16[136,1024]{1,0:T(8,128)(2,1)} %get-tuple-element.33.x_hbm), channel_id=1, source_target_pairs={{0,8},{8,16},{16,24},{24,32},{32,40},{40,48},{48,56},{56,64},{64,7... | collective-permute-start | bytes 835592 | tf_op jit(solution)/shard_map/ppermute | solution.py:460
  12.2 14.7 %collective-permute-done.x_hbm = bf16[136,1024]{1,0:T(8,128)(2,1)} collective-permute-done((bf16[136,1024]{1,0:T(8,128)(2,1)}, bf16[136,1024]{1,0:T(8,128)(2,1)}, u32[]{:S(2)}, u32[]{:S(2)}) %collective-permute-start) | collective-permute-done | bytes 278560 | tf_op jit(solution)/shard_map/ppermute | solution.py:460
  26.9 3.7 %project_prev.1 = bf16[8,136,256]{2,1,0:T(8,128)(2,1)} custom-call(s32[192]{0:T(256)} %counts_hbm.3, bf16[136,1024]{1,0:T(8,128)(2,1)} %collective-permute-done.x_hbm, bf16[1024,4096]{1,0:T(8,128)(2,1)} %w_hbm.5), custom_call_target="tpu_custom_call" | custom-call | flops 536870912 | bytes 4194304 | tf_op jit(solution)/shard_map/project_prev/pallas_call | solution.py:175
  30.6 0.0 all-to-all-done.1
  30.6 0.0 copy-done.3
  30.6 14.9 %conditional.1 = (bf16[2,1024,256]{2,1,0:T(8,128)(2,1)}, f32[1024,128]{1,0:T(8,128)}, bf16[8,136,256]{2,1,0:T(8,128)(2,1)}) conditional(s32[]{:T(128)} %convert_element_type.3, (bf16[8,136,384]{2,1,0:T(8,128)(2,1)}, f32[16,64]{1,0:T(8,128)S(1)}, bf16[8,136,256]{2,1,0:T(8,128)(2,1)}) %tuple.16, (bf16[8,136,384]{2,1,0:T(8,128)(2,1)}, ...), branch_computations={%region_0.0_spmd, %region_1.0_spmd} | conditional | flops 1073741824 | bytes 5865528 | solution.py:474
  30.6 4.4 %all-to-all-start = ((bf16[8,136,256]{2,1,0:T(8,128)(2,1)}), bf16[8,136,256]{2,1,0:T(8,128)(2,1)}, u32[]{:S(2)}, u32[]{:S(2)}) async-start(bf16[8,136,256]{2,1,0:T(8,128)(2,1)} %get-tuple-element.21), calls=%async_computation | async-start | bytes 1114112 | tf_op jit(solution)/shard_map/cond/branch_0_fun/all_to_all | solution.py:452
  35.0 5.2 %attend_own.2 = (bf16[2,1024,256]{2,1,0:T(8,128)(2,1)}, f32[1024,128]{1,0:T(8,128)}) custom-call(bf16[8,136,384]{2,1,0:T(8,128)(2,1)} %get-tuple-element.17.own_ref, f32[16,64]{1,0:T(8,128)S(1)} %get-tuple-element.18.bias_ref), custom_call_target="tpu_custom_call" | custom-call | flops 1073741824 | bytes 4194304 | tf_op jit(solution)/shard_map/cond/branch_0_fun/attend_own/pallas_call | solution.py:319
  40.2 5.3 %all-to-all-done = bf16[8,136,256]{2,1,0:T(8,128)(2,1)} async-done(((bf16[8,136,256]{2,1,0:T(8,128)(2,1)}), bf16[8,136,256]{2,1,0:T(8,128)(2,1)}, u32[]{:S(2)}, u32[]{:S(2)}) %all-to-all-start) | async-done | bytes 557088 | tf_op jit(solution)/shard_map/cond/branch_0_fun/all_to_all | solution.py:452
  45.5 4.8 %attend_prev.1 = bf16[8,128,128]{2,1,0:T(8,128)(2,1)} custom-call(bf16[2,1024,256]{2,1,0:T(8,128)(2,1)} %get-tuple-element.34.left_hbm, f32[1024,128]{1,0:T(8,128)} %get-tuple-element.35.sum_hbm, bf16[8,136,256]{2,1,0:T(8,128)(2,1)} %get-tuple-element.36.prev_hbm, bf16[1024,256]{1,0:T(8,128)(2,1)} %cache_k.1, bf16[1024,256]{1,0:T(8,128)(2,1)} %cache_v.1, ...), custom_call_target="tpu_custom_call" | custom-call | flops 4294967296 | bytes 4194304 | tf_op jit(solution)/shard_map/attend_prev/pallas_call | solution.py:405
  50.3 4.1 %all-to-all-start.2 = ((bf16[8,128,128]{2,1,0:T(8,128)(2,1)}), bf16[8,128,128]{2,1,0:T(8,128)(2,1)}, u32[]{:S(2)}, u32[]{:S(2)}) async-start(bf16[8,128,128]{2,1,0:T(8,128)(2,1)} %attend_prev.1), calls=%async_computation.2 | async-start | bytes 524288 | tf_op jit(solution)/shard_map/all_to_all | solution.py:452
  54.3 2.9 %project_u.1.gate_ref = bf16[128,1024]{1,0:T(8,128)(2,1)} custom-call(bf16[136,1024]{1,0:T(8,128)(2,1)} %get-tuple-element.33.x_hbm, bf16[1024,4096]{1,0:T(8,128)(2,1)} %w_hbm.5), custom_call_target="tpu_custom_call" | custom-call | flops 268435456 | bytes 2097152 | tf_op jit(solution)/shard_map/project_u/pallas_call | solution.py:210
  57.2 4.3 %all-to-all-done.2.attended_ref = bf16[8,128,128]{2,1,0:T(8,128)(2,1)} async-done(((bf16[8,128,128]{2,1,0:T(8,128)(2,1)}), bf16[8,128,128]{2,1,0:T(8,128)(2,1)}, u32[]{:S(2)}, u32[]{:S(2)}) %all-to-all-start.2) | async-done | bytes 262176 | tf_op jit(solution)/shard_map/all_to_all | solution.py:452
  61.6 0.0 copy-start
  61.6 1.6 %copy-done = bf16[1024,1024]{1,0:T(8,128)(2,1)S(1)} copy-done((bf16[1024,1024]{1,0:T(8,128)(2,1)S(1)}, bf16[1024,1024]{1,0:T(8,128)(2,1)}, u32[]{:S(2)}) %copy-start) | copy-done | bytes 2097176
  63.2 0.0 copy-start.1
  63.2 0.9 %copy-done.1 = bf16[128,1024]{1,0:T(8,128)(2,1)S(1)} copy-done((bf16[128,1024]{1,0:T(8,128)(2,1)S(1)}, bf16[128,1024]{1,0:T(8,128)(2,1)}, u32[]{:S(2)}) %copy-start.1) | copy-done | bytes 262168
  64.1 0.0 copy-start.2
  64.1 0.9 %copy-done.2 = bf16[128,1024]{1,0:T(8,128)(2,1)S(1)} copy-done((bf16[128,1024]{1,0:T(8,128)(2,1)S(1)}, bf16[128,1024]{1,0:T(8,128)(2,1)}, u32[]{:S(2)}) %copy-start.2) | copy-done | bytes 262168
  65.1 2.3 %mix.1 = bf16[128,1024]{1,0:T(8,128)(2,1)} custom-call(bf16[8,128,128]{2,1,0:T(8,128)(2,1)} %all-to-all-done.2.attended_ref, bf16[128,1024]{1,0:T(8,128)(2,1)S(1)} %copy-done.2, bf16[128,1024]{1,0:T(8,128)(2,1)S(1)} %copy-done.1, bf16[1024,1024]{1,0:T(8,128)(2,1)S(1)} %copy-done), custom_call_target="tpu_custom_call" | custom-call | flops 268435456 | bytes 3145728 | tf_op jit(solution)/shard_map/mix/pallas_call | solution.py:440
Async XLA Ops:
  0.0 30.6 %copy-start.3 = (f32[64,16]{0,1:T(8,128)S(1)}, f32[64,16]{0,1:T(8,128)}, u32[]{:S(2)}) copy-start(f32[64,16]{0,1:T(8,128)} %param.19) | copy-start | bytes 12292
  4.4 26.1 %all-to-all-start.1 = ((bf16[8,136,384]{2,1,0:T(8,128)(2,1)}), bf16[8,136,384]{2,1,0:T(8,128)(2,1)}, u32[]{:S(2)}, u32[]{:S(2)}) async-start(bf16[8,136,384]{2,1,0:T(8,128)(2,1)} %get-tuple-element.32), calls=%async_computation.1 | async-start | bytes 1671168 | tf_op jit(solution)/shard_map/all_to_all | solution.py:452
  8.7 18.1 %collective-permute-start = (bf16[136,1024]{1,0:T(8,128)(2,1)}, bf16[136,1024]{1,0:T(8,128)(2,1)}, u32[]{:S(2)}, u32[]{:S(2)}) collective-permute-start(bf16[136,1024]{1,0:T(8,128)(2,1)} %get-tuple-element.33.x_hbm), channel_id=1, source_target_pairs={{0,8},{8,16},{16,24},{24,32},{32,40},{40,48},{48,56},{56,64},{64,7... | collective-permute-start | bytes 835592 | tf_op jit(solution)/shard_map/ppermute | solution.py:460
  30.6 14.9 %all-to-all-start = ((bf16[8,136,256]{2,1,0:T(8,128)(2,1)}), bf16[8,136,256]{2,1,0:T(8,128)(2,1)}, u32[]{:S(2)}, u32[]{:S(2)}) async-start(bf16[8,136,256]{2,1,0:T(8,128)(2,1)} %get-tuple-element.21), calls=%async_computation | async-start | bytes 1114112 | tf_op jit(solution)/shard_map/cond/branch_0_fun/all_to_all | solution.py:452
  50.3 11.3 %all-to-all-start.2 = ((bf16[8,128,128]{2,1,0:T(8,128)(2,1)}), bf16[8,128,128]{2,1,0:T(8,128)(2,1)}, u32[]{:S(2)}, u32[]{:S(2)}) async-start(bf16[8,128,128]{2,1,0:T(8,128)(2,1)} %attend_prev.1), calls=%async_computation.2 | async-start | bytes 524288 | tf_op jit(solution)/shard_map/all_to_all | solution.py:452
  61.6 1.6 %copy-start = (bf16[1024,1024]{1,0:T(8,128)(2,1)S(1)}, bf16[1024,1024]{1,0:T(8,128)(2,1)}, u32[]{:S(2)}) copy-start(bf16[1024,1024]{1,0:T(8,128)(2,1)} %w_ref.1) | copy-start | bytes 6291460
  63.2 0.9 %copy-start.1 = (bf16[128,1024]{1,0:T(8,128)(2,1)S(1)}, bf16[128,1024]{1,0:T(8,128)(2,1)}, u32[]{:S(2)}) copy-start(bf16[128,1024]{1,0:T(8,128)(2,1)} %events_ref.1) | copy-start | bytes 786436
  64.1 0.9 %copy-start.2 = (bf16[128,1024]{1,0:T(8,128)(2,1)S(1)}, bf16[128,1024]{1,0:T(8,128)(2,1)}, u32[]{:S(2)}) copy-start(bf16[128,1024]{1,0:T(8,128)(2,1)} %project_u.1.gate_ref) | copy-start | bytes 786436

commit v4 on v2

--- a/solution.py
+++ b/solution.py
@@ -50,6 +50,7 @@
 
 STARTS = {"u": 0, "v": 1024, "q": 2048, "k": 3072}
 ALL = 67_000_000
+LAST = 53
 
 
 def weight_copies(w_hbm, ws, sems, kinds):
@@ -331,72 +332,95 @@
     )(own, bias_rows_in)
 
 
+def cache_kernel(cache_k, cache_v, cache_b, out_hbm, buckets, out, sems, out_sem):
+    start = pl.multiple_of(lax.axis_index("side") * LANES, LANES)
+    copies = [pltpu.make_async_copy(cache_b, buckets, sems.at[16])]
+    for s in range(8):
+        for place, cache in enumerate((cache_k, cache_v)):
+            block = cache.at[pl.ds(s * ROWS, ROWS), pl.ds(start, LANES)]
+            into = out.at[s, pl.ds(0, ROWS), pl.ds(place * LANES, LANES)]
+            copies.append(pltpu.make_async_copy(block, into, sems.at[2 * s + place]))
+    started(*copies)
+    copies[0].wait()
+    for s in range(8):
+        row = buckets[s : s + 1, :].astype(F32)
+        tail = jnp.broadcast_to(jnp.concatenate([row, row], axis=1), (EXT - ROWS, 2 * LANES))
+        out[s, ROWS:EXT, :] = tail.astype(BF16)
+    for copy in copies[1:]:
+        copy.wait()
+    send = pltpu.make_async_copy(out, out_hbm, out_sem)
+    send.start()
+    send.wait()
+
+
+def cache_call(prior_keys, prior_values, prior_buckets):
+    shape = (8, EXT, 2 * LANES)
+    return pl.pallas_call(
+        cache_kernel,
+        out_shape=jax.ShapeDtypeStruct(shape, BF16),
+        in_specs=[hbm()] * 3,
+        out_specs=hbm(),
+        scratch_shapes=[
+            pltpu.VMEM((8, LANES), jnp.int32),
+            pltpu.VMEM(shape, BF16),
+            pltpu.SemaphoreType.DMA((17,)),
+            pltpu.SemaphoreType.DMA,
+        ],
+        cost_estimate=cost(0, 2 << 20),
+        compiler_params=pltpu.CompilerParams(vmem_limit_bytes=ALL),
+        name="cached_blocks",
+    )(prior_keys, prior_values, prior_buckets)
+
+
 def attend_prev_kernel(
-    left_hbm, sum_hbm, prev_hbm, cache_k, cache_v, cache_b, out_hbm,
-    left_ref, sum_ref, prev_ref, out_ref, keys, values, rows, hot, sems, in_sems, out_sems
+    left_hbm, sum_hbm, prev_hbm, out_hbm, left_ref, sum_ref, prev_ref, out_ref, hot, in_sems, out_sems
 ):
-    first = lax.axis_index("outer") == 0
-    prev_copy, left_copy, sum_copy = started(
-        pltpu.make_async_copy(prev_hbm, prev_ref, in_sems.at[0]),
-        pltpu.make_async_copy(left_hbm, left_ref, in_sems.at[1]),
-        pltpu.make_async_copy(sum_hbm, sum_ref, in_sems.at[2]),
-    )
+    prev_copy = pltpu.make_async_copy(prev_hbm, prev_ref, in_sems.at[8])
+    prev_copy.start()
+    tiles = []
+    for i in range(4):
+        rows = pl.ds(i * TILE, TILE)
+        tiles.append(
+            started(
+                pltpu.make_async_copy(left_hbm.at[:, rows], left_ref.at[:, rows], in_sems.at[2 * i]),
+                pltpu.make_async_copy(sum_hbm.at[rows], sum_ref.at[rows], in_sems.at[2 * i + 1]),
+            )
+        )
     prev_copy.wait()
-
-    @pl.when(first)
-    def _():
-        start = pl.multiple_of(lax.axis_index("side") * LANES, LANES)
-        copies = started(
-            pltpu.make_async_copy(cache_k.at[:, pl.ds(start, LANES)], keys, sems.at[0]),
-            pltpu.make_async_copy(cache_v.at[:, pl.ds(start, LANES)], values, sems.at[1]),
-            pltpu.make_async_copy(cache_b, rows, sems.at[2]),
-        )
-        for copy in copies:
-            copy.wait()
-
-    @pl.when(jnp.logical_not(first))
-    def _():
-        for s in range(8):
-            at = slice(s * LANES, (s + 1) * LANES)
-            rows[s : s + 1, :] = prev_ref[s, ROWS : ROWS + 1, 0:LANES].astype(F32).astype(jnp.int32)
-            keys[at, :] = prev_ref[s, 0:ROWS, 0:LANES]
-            values[at, :] = prev_ref[s, 0:ROWS, LANES : 2 * LANES]
-
     for s in range(8):
         at = slice(s * LANES, (s + 1) * LANES)
-        hot[at, :] = hot_of(rows[s : s + 1, :].astype(F32))
-    left_copy.wait()
-    sum_copy.wait()
+        hot[at, :] = hot_of(prev_ref[s, ROWS : ROWS + 1, 0:LANES].astype(F32))
     lane = lax.broadcasted_iota(jnp.int32, (TILE, LANES), 1)
     sends = []
-    for b in range(2):
-        for t in range(2):
-            start = b * 512 + t * TILE
-            at = slice(start, start + TILE)
-            sums = []
-            for j in range(2):
-                total = None
-                for begin in (0, 512) if b == 0 else (512,):
-                    span = slice(begin, begin + 512)
-                    part = attended_sum(left_ref[j, at, :], keys[span, :], hot[span, :], values[span, :])
-                    total = part if total is None else total + part
-                sums.append(total)
-            whole = sum_ref[at, :] + jnp.where(lane < NB, sums[0], sums[1])
-            s = start // LANES
-            out_ref[s : s + 2, :, :] = whole.astype(BF16).reshape(2, LANES, LANES)
-            two = pl.ds(s, 2)
-            sends += started(
-                pltpu.make_async_copy(out_ref.at[two], out_hbm.at[two], out_sems.at[s // 2])
-            )
+    for i in range(4):
+        at = slice(i * TILE, (i + 1) * TILE)
+        for copy in tiles[i]:
+            copy.wait()
+        sums = []
+        for j in range(2):
+            total = None
+            for begin in (0, 512) if i < 2 else (512,):
+                part = attended_sum(
+                    left_ref[j, at, :],
+                    part_of(prev_ref, begin, 512, 0),
+                    hot[begin : begin + 512, :],
+                    part_of(prev_ref, begin, 512, 1),
+                )
+                total = part if total is None else total + part
+            sums.append(total)
+        whole = sum_ref[at, :] + jnp.where(lane < NB, sums[0], sums[1])
+        out_ref[2 * i : 2 * i + 2, :, :] = whole.astype(BF16).reshape(2, LANES, LANES)
+        two = pl.ds(2 * i, 2)
+        sends += started(pltpu.make_async_copy(out_ref.at[two], out_hbm.at[two], out_sems.at[i]))
     for copy in sends:
         copy.wait()
 
 
-def attend_prev_call(left, partial, prev, prior_keys, prior_values, prior_buckets):
+def attend_prev_call(left, partial, prev):
     return pl.pallas_call(
         attend_prev_kernel,
         out_shape=jax.ShapeDtypeStruct((8, ROWS, LANES), BF16),
-        in_specs=[hbm()] * 6,
+        in_specs=[hbm()] * 3,
         out_specs=hbm(),
         scratch_shapes=[
             pltpu.VMEM(left.shape, BF16),
@@ -404,17 +428,13 @@
             pltpu.VMEM(prev.shape, BF16),
             pltpu.VMEM((8, ROWS, LANES), BF16),
             pltpu.VMEM((1024, LANES), BF16),
-            pltpu.VMEM((1024, LANES), BF16),
-            pltpu.VMEM((8, LANES), jnp.int32),
-            pltpu.VMEM((1024, LANES), BF16),
-            pltpu.SemaphoreType.DMA((3,)),
-            pltpu.SemaphoreType.DMA((3,)),
+            pltpu.SemaphoreType.DMA((9,)),
             pltpu.SemaphoreType.DMA((4,)),
         ],
         cost_estimate=cost(4 * 1024 * 1024 * 1024, 4 << 20),
-        compiler_params=pltpu.CompilerParams(vmem_limit_bytes=61 << 20),
+        compiler_params=limited(LAST),
         name="attend_prev",
-    )(left, partial, prev, prior_keys, prior_values, prior_buckets)
+    )(left, partial, prev)
 
 
 def mix_kernel(attended_ref, gate_ref, events_ref, w_ref, out_ref):
@@ -452,11 +472,21 @@
     own = exchanged(sent)
     gate = gate_call(normed, w_input)
     sent = project_prev_call(earlier, counts, w_input)
-    prev = exchanged(sent)
-    left, partial = attend_own_call(own, time_bias.T)
-    attended = attend_prev_call(
-        left, partial, prev, prior_keys, prior_values, prior_buckets.reshape(8, LANES)
-    )
+
+    def cached(own, sent, bias, *prior):
+        left, partial = attend_own_call(own, bias)
+        return left, partial, cache_call(*prior)
+
+    def received(own, sent, bias, *prior):
+        prev = exchanged(sent)
+        left, partial = attend_own_call(own, bias)
+        return left, partial, prev
+
+    prior = (prior_keys, prior_values, prior_buckets.reshape(8, LANES))
+    left, partial, prev = lax.cond(
+        lax.axis_index("outer") == 0, cached, received, own, sent, time_bias.T, *prior
+    )
+    attended = attend_prev_call(left, partial, prev)
     attended = exchanged(attended)
     return mix_call(attended, gate, events, w_output)
 

time: 69.5 us -> 68.4 us (0.984)
  the two profiles are of different devices: /device:TPU:1 before, /device:TPU:8 now
where the time goes in v4:
time: 68.4 us; the launch traced here: 67.8 us
  waiting for transfers between devices  24.3 us (36%)
  Pallas kernels  23.6 us (35%)
  starting transfers between devices  16.3 us (24%)
  local copies, waits for them, and re-layouts  3.5 us (5%)
    ppermute x1, waiting for transfers between devices, per_device(): lax.ppermute(normed, 'outer', [(i, i + 1) for i in range(outer - 1)])  14.6 us
    all_to_all x3, starting transfers between devices, exchanged(): return lax.all_to_all(parts, RING, split_axis=0, concat_axis=0, tiled=True)  12.8 us
    all_to_all x3, waiting for transfers between devices, exchanged(): return lax.all_to_all(parts, RING, split_axis=0, concat_axis=0, tiled=True)  9.65 us
    pallas_call x1, Pallas kernels, attend_own_call(): pl.pallas_call(attend_own_kernel, out_shape=(jax.ShapeDtypeStruct((2, 102...  5.17 us
    pallas_call x1, Pallas kernels, attend_prev_call(): pl.pallas_call(attend_prev_kernel, out_shape=jax.ShapeDtypeStruct((8, ROW...  5.12 us
    pallas_call x1, Pallas kernels, project_call(): pl.pallas_call(project_kernel, out_shape=(jax.ShapeDtypeStruct((EXT, dept...  4.44 us
    pallas_call x1, Pallas kernels, project_prev_call(): pl.pallas_call(project_prev_kernel, out_shape=jax.ShapeDtypeStruct((8, EX...  3.68 us
    unnamed x10, local copies, waits for them, and re-layouts  3.5 us
  transfers between devices with their start and end apart: 4, of which 3 were waited for; matrix products, arithmetic and copies ran while one was open for 0% of the time, Pallas kernels for 17%

profile of v4, /device:TPU:8, one launch (start us, length us, event | category | flops | bytes accessed | tf_op | source)
XLA Modules:
  0.0 67.8 jit_solution(12173163006801178445)
XLA Ops:
  0.0 0.0 copy-start.3
  0.0 0.0 copy-start.4
  0.0 4.4 %project_own.1 = (bf16[136,1024]{1,0:T(8,128)(2,1)}, bf16[8,136,384]{2,1,0:T(8,128)(2,1)}) custom-call(bf16[128,1024]{1,0:T(8,128)(2,1)} %events_ref.1, s32[4,128]{1,0:T(4,128)} %bitcast.4, s32[192]{0:T(256)} %counts_hbm.3, bf16[1024,4096]{1,0:T(8,128)(2,1)} %w_hbm.5), custom_call_target="tpu_custom_call" | custom-call | flops 1073741824 | bytes 8388608 | tf_op jit(solution)/shard_map/project_own/pallas_call | solution.py:126
  4.5 4.3 %all-to-all-start.1 = ((bf16[8,136,384]{2,1,0:T(8,128)(2,1)}), bf16[8,136,384]{2,1,0:T(8,128)(2,1)}, u32[]{:S(2)}, u32[]{:S(2)}) async-start(bf16[8,136,384]{2,1,0:T(8,128)(2,1)} %get-tuple-element.39), calls=%async_computation.1 | async-start | bytes 1671168 | tf_op jit(solution)/shard_map/all_to_all | solution.py:463
  8.8 3.5 %collective-permute-start = (bf16[136,1024]{1,0:T(8,128)(2,1)}, bf16[136,1024]{1,0:T(8,128)(2,1)}, u32[]{:S(2)}, u32[]{:S(2)}) collective-permute-start(bf16[136,1024]{1,0:T(8,128)(2,1)} %get-tuple-element.40.x_hbm), channel_id=1, source_target_pairs={{0,8},{8,16},{16,24},{24,32},{32,40},{40,48},{48,56},{56,64},{64,7... | collective-permute-start | bytes 835592 | tf_op jit(solution)/shard_map/ppermute | solution.py:471
  12.3 14.6 %collective-permute-done.x_hbm = bf16[136,1024]{1,0:T(8,128)(2,1)} collective-permute-done((bf16[136,1024]{1,0:T(8,128)(2,1)}, bf16[136,1024]{1,0:T(8,128)(2,1)}, u32[]{:S(2)}, u32[]{:S(2)}) %collective-permute-start) | collective-permute-done | bytes 278560 | tf_op jit(solution)/shard_map/ppermute | solution.py:471
  26.9 3.7 %project_prev.1 = bf16[8,136,256]{2,1,0:T(8,128)(2,1)} custom-call(s32[192]{0:T(256)} %counts_hbm.3, bf16[136,1024]{1,0:T(8,128)(2,1)} %collective-permute-done.x_hbm, bf16[1024,4096]{1,0:T(8,128)(2,1)} %w_hbm.5), custom_call_target="tpu_custom_call" | custom-call | flops 536870912 | bytes 4194304 | tf_op jit(solution)/shard_map/project_prev/pallas_call | solution.py:176
  30.6 0.0 all-to-all-done.1
  30.6 0.0 copy-done.3
  30.6 0.0 copy-done.4
  30.6 14.9 %conditional.1 = (bf16[2,1024,256]{2,1,0:T(8,128)(2,1)}, f32[1024,128]{1,0:T(8,128)}, bf16[8,136,256]{2,1,0:T(8,128)(2,1)}) conditional(s32[]{:T(128)} %convert_element_type.3, (bf16[8,136,384]{2,1,0:T(8,128)(2,1)}, f32[16,64]{1,0:T(8,128)S(1)}, bf16[8,136,256]{2,1,0:T(8,128)(2,1)}) %tuple.18, (bf16[8,136,384]{2,1,0:T(8,128)(2,1)}, ...), branch_computations={%region_0.0_spmd, %region_1.0_spmd} | conditional | flops 1073741824 | bytes 6291480 | solution.py:486
  30.6 4.4 %all-to-all-start = ((bf16[8,136,256]{2,1,0:T(8,128)(2,1)}), bf16[8,136,256]{2,1,0:T(8,128)(2,1)}, u32[]{:S(2)}, u32[]{:S(2)}) async-start(bf16[8,136,256]{2,1,0:T(8,128)(2,1)} %get-tuple-element.26), calls=%async_computation | async-start | bytes 1114112 | tf_op jit(solution)/shard_map/cond/branch_0_fun/all_to_all | solution.py:463
  35.1 5.2 %attend_own.2 = (bf16[2,1024,256]{2,1,0:T(8,128)(2,1)}, f32[1024,128]{1,0:T(8,128)}) custom-call(bf16[8,136,384]{2,1,0:T(8,128)(2,1)} %get-tuple-element.22.own_ref, f32[16,64]{1,0:T(8,128)S(1)} %get-tuple-element.23.bias_ref), custom_call_target="tpu_custom_call" | custom-call | flops 1073741824 | bytes 4194304 | tf_op jit(solution)/shard_map/cond/branch_0_fun/attend_own/pallas_call | solution.py:320
  40.2 5.3 %all-to-all-done = bf16[8,136,256]{2,1,0:T(8,128)(2,1)} async-done(((bf16[8,136,256]{2,1,0:T(8,128)(2,1)}), bf16[8,136,256]{2,1,0:T(8,128)(2,1)}, u32[]{:S(2)}, u32[]{:S(2)}) %all-to-all-start) | async-done | bytes 557088 | tf_op jit(solution)/shard_map/cond/branch_0_fun/all_to_all | solution.py:463
  45.6 5.1 %attend_prev.1 = bf16[8,128,128]{2,1,0:T(8,128)(2,1)} custom-call(bf16[2,1024,256]{2,1,0:T(8,128)(2,1)} %get-tuple-element.41.left_hbm, f32[1024,128]{1,0:T(8,128)} %get-tuple-element.42.sum_hbm, bf16[8,136,256]{2,1,0:T(8,128)(2,1)} %get-tuple-element.43.prev_hbm), custom_call_target="tpu_custom_call" | custom-call | flops 4294967296 | bytes 4194304 | tf_op jit(solution)/shard_map/attend_prev/pallas_call | solution.py:420
  50.7 4.1 %all-to-all-start.2 = ((bf16[8,128,128]{2,1,0:T(8,128)(2,1)}), bf16[8,128,128]{2,1,0:T(8,128)(2,1)}, u32[]{:S(2)}, u32[]{:S(2)}) async-start(bf16[8,128,128]{2,1,0:T(8,128)(2,1)} %attend_prev.1), calls=%async_computation.2 | async-start | bytes 524288 | tf_op jit(solution)/shard_map/all_to_all | solution.py:463
  54.7 2.9 %project_u.1.gate_ref = bf16[128,1024]{1,0:T(8,128)(2,1)} custom-call(bf16[136,1024]{1,0:T(8,128)(2,1)} %get-tuple-element.40.x_hbm, bf16[1024,4096]{1,0:T(8,128)(2,1)} %w_hbm.5), custom_call_target="tpu_custom_call" | custom-call | flops 268435456 | bytes 2097152 | tf_op jit(solution)/shard_map/project_u/pallas_call | solution.py:211
  57.6 4.3 %all-to-all-done.2.attended_ref = bf16[8,128,128]{2,1,0:T(8,128)(2,1)} async-done(((bf16[8,128,128]{2,1,0:T(8,128)(2,1)}), bf16[8,128,128]{2,1,0:T(8,128)(2,1)}, u32[]{:S(2)}, u32[]{:S(2)}) %all-to-all-start.2) | async-done | bytes 262176 | tf_op jit(solution)/shard_map/all_to_all | solution.py:463
  62.0 0.0 copy-start
  62.0 1.6 %copy-done = bf16[1024,1024]{1,0:T(8,128)(2,1)S(1)} copy-done((bf16[1024,1024]{1,0:T(8,128)(2,1)S(1)}, bf16[1024,1024]{1,0:T(8,128)(2,1)}, u32[]{:S(2)}) %copy-start) | copy-done | bytes 2097176
  63.6 0.0 copy-start.1
  63.6 0.9 %copy-done.1 = bf16[128,1024]{1,0:T(8,128)(2,1)S(1)} copy-done((bf16[128,1024]{1,0:T(8,128)(2,1)S(1)}, bf16[128,1024]{1,0:T(8,128)(2,1)}, u32[]{:S(2)}) %copy-start.1) | copy-done | bytes 262168
  64.5 0.0 copy-start.2
  64.5 0.9 %copy-done.2 = bf16[128,1024]{1,0:T(8,128)(2,1)S(1)} copy-done((bf16[128,1024]{1,0:T(8,128)(2,1)S(1)}, bf16[128,1024]{1,0:T(8,128)(2,1)}, u32[]{:S(2)}) %copy-start.2) | copy-done | bytes 262168
  65.5 2.3 %mix.1 = bf16[128,1024]{1,0:T(8,128)(2,1)} custom-call(bf16[8,128,128]{2,1,0:T(8,128)(2,1)} %all-to-all-done.2.attended_ref, bf16[128,1024]{1,0:T(8,128)(2,1)S(1)} %copy-done.2, bf16[128,1024]{1,0:T(8,128)(2,1)S(1)} %copy-done.1, bf16[1024,1024]{1,0:T(8,128)(2,1)S(1)} %copy-done), custom_call_target="tpu_custom_call" | custom-call | flops 268435456 | bytes 3145728 | tf_op jit(solution)/shard_map/mix/pallas_call | solution.py:451
Async XLA Ops:
  0.0 30.6 %copy-start.3 = (s32[1024]{0:T(1024)S(1)}, s32[1024]{0:T(1024)}, u32[]{:S(2)}) copy-start(s32[1024]{0:T(1024)} %param.16) | copy-start | bytes 12292
  0.0 30.6 %copy-start.4 = (f32[64,16]{0,1:T(8,128)S(1)}, f32[64,16]{0,1:T(8,128)}, u32[]{:S(2)}) copy-start(f32[64,16]{0,1:T(8,128)} %param.19) | copy-start | bytes 12292
  4.5 26.1 %all-to-all-start.1 = ((bf16[8,136,384]{2,1,0:T(8,128)(2,1)}), bf16[8,136,384]{2,1,0:T(8,128)(2,1)}, u32[]{:S(2)}, u32[]{:S(2)}) async-start(bf16[8,136,384]{2,1,0:T(8,128)(2,1)} %get-tuple-element.39), calls=%async_computation.1 | async-start | bytes 1671168 | tf_op jit(solution)/shard_map/all_to_all | solution.py:463
  8.8 18.1 %collective-permute-start = (bf16[136,1024]{1,0:T(8,128)(2,1)}, bf16[136,1024]{1,0:T(8,128)(2,1)}, u32[]{:S(2)}, u32[]{:S(2)}) collective-permute-start(bf16[136,1024]{1,0:T(8,128)(2,1)} %get-tuple-element.40.x_hbm), channel_id=1, source_target_pairs={{0,8},{8,16},{16,24},{24,32},{32,40},{40,48},{48,56},{56,64},{64,7... | collective-permute-start | bytes 835592 | tf_op jit(solution)/shard_map/ppermute | solution.py:471
  30.6 14.9 %all-to-all-start = ((bf16[8,136,256]{2,1,0:T(8,128)(2,1)}), bf16[8,136,256]{2,1,0:T(8,128)(2,1)}, u32[]{:S(2)}, u32[]{:S(2)}) async-start(bf16[8,136,256]{2,1,0:T(8,128)(2,1)} %get-tuple-element.26), calls=%async_computation | async-start | bytes 1114112 | tf_op jit(solution)/shard_map/cond/branch_0_fun/all_to_all | solution.py:463
  50.7 11.3 %all-to-all-start.2 = ((bf16[8,128,128]{2,1,0:T(8,128)(2,1)}), bf16[8,128,128]{2,1,0:T(8,128)(2,1)}, u32[]{:S(2)}, u32[]{:S(2)}) async-start(bf16[8,128,128]{2,1,0:T(8,128)(2,1)} %attend_prev.1), calls=%async_computation.2 | async-start | bytes 524288 | tf_op jit(solution)/shard_map/all_to_all | solution.py:463
  62.0 1.6 %copy-start = (bf16[1024,1024]{1,0:T(8,128)(2,1)S(1)}, bf16[1024,1024]{1,0:T(8,128)(2,1)}, u32[]{:S(2)}) copy-start(bf16[1024,1024]{1,0:T(8,128)(2,1)} %w_ref.1) | copy-start | bytes 6291460
  63.6 0.9 %copy-start.1 = (bf16[128,1024]{1,0:T(8,128)(2,1)S(1)}, bf16[128,1024]{1,0:T(8,128)(2,1)}, u32[]{:S(2)}) copy-start(bf16[128,1024]{1,0:T(8,128)(2,1)} %events_ref.1) | copy-start | bytes 786436
  64.5 0.9 %copy-start.2 = (bf16[128,1024]{1,0:T(8,128)(2,1)S(1)}, bf16[128,1024]{1,0:T(8,128)(2,1)}, u32[]{:S(2)}) copy-start(bf16[128,1024]{1,0:T(8,128)(2,1)} %project_u.1.gate_ref) | copy-start | bytes 786436
